TPU v7x, 32 devices: a whole 2x2x4 slice. The times are simulated.
32 devices in a mesh: level: 8 (over y, x, core), slab: 4 (over z).
Axes of the slice: x: 2, y: 2, z: 4, core: 2. Of those that a mesh axis runs over, the one named last changes fastest.
Arguments:
- right_side: float32 [16, 128, 512], P('slab', 'level'), may hold values from -6 to 6
- scale_field: float32 [16, 128, 512], P('slab', 'level'), may hold values from 0.7 to 1.4
- mass_field: float32 [16, 128, 512], P('slab', 'level'), may hold values from 0.05 to 0.5
- degrees: int32 [3], replicated, may hold values from 2 to 6, as said below
- lower_bound: float32 [3], replicated, may hold values from 0.05 to 0.3
- upper_bound: float32 [3], replicated, may hold values from 2 to 2.6
Outputs:
- solution: float32 [16, 128, 512], P('slab', 'level')
- final_res: float32 [16, 128, 512], P('slab', 'level')
Inputs may be any that keep to these rules, and one draw needn't show every extreme that they name: `degrees`: degree of each grid; in every draw at least one grid has degree exactly 6.
All inputs are finite; a program needn't handle non-finite values.
Results may differ from a plain program's by a relative error of at most 0.0001.
Values sent between devices are 32-bit elements; how exact they have to be, the bound alone decides.
No kernel may reach another device: no remote copies, remote signals or barrier semaphores. Data moves between devices by JAX's collectives and lax.ppermute only.
A program may use at most 128 MiB of HBM per device.

v0:
```python
import math

import jax
import jax.numpy as jnp
from jax import lax
from jax.experimental import pallas as pl
from jax.experimental.pallas import tpu as pltpu
from jax.sharding import PartitionSpec as P


CYCLES = 3
MAXDEG = 6
INTERPRET = False

F32 = jnp.float32
OUT = 8
XH = 6
MH = 6
LH = 6
YH = 64


def dot(a, b):
    return jnp.dot(a, b, precision=lax.Precision.HIGHEST, preferred_element_type=F32)


def blocks(ref, rows):
    return jnp.concatenate([ref[b, rows, :] for b in range(ref.shape[0])], axis=1)


def put_blocks(ref, rows, value):
    for b in range(ref.shape[0]):
        ref[b, rows, :] = value[:, 128 * b : 128 * b + 128]


def iota(shape, dim):
    return lax.broadcasted_iota(jnp.int32, shape, dim)


def zy_sum(w, nz):
    rows, lanes = w.shape
    if nz % 8 == 0:
        v = w.reshape(rows // nz, nz // 8, 8, lanes)
        at = iota(v.shape, 2)
        edge = jnp.zeros_like(v[:, :1])
        up = pltpu.roll(w.reshape(rows // 8, 8, lanes), 1, 1).reshape(v.shape)
        down = pltpu.roll(w.reshape(rows // 8, 8, lanes), 7, 1).reshape(v.shape)
        up_over = down_over = edge
        if nz > 8:
            up_over = jnp.concatenate([edge, up[:, :-1]], axis=1)
            down_over = jnp.concatenate([down[:, 1:], edge], axis=1)
        s = v + jnp.where(at == 0, up_over, up) + jnp.where(at == 7, down_over, down)
        s = s.reshape(rows, lanes)
    else:
        at = iota(w.shape, 0) & (nz - 1)
        up = jnp.where(at == 0, 0.0, pltpu.roll(w, 1, 0))
        down = jnp.where(at == nz - 1, 0.0, pltpu.roll(w, rows - 1, 0))
        s = w + up + down
    at = iota((rows, 128), 1)
    n = lanes // 128
    part = [s[:, 128 * b : 128 * b + 128] for b in range(n)]
    left = [pltpu.roll(p, 1, 1) for p in part]
    right = [pltpu.roll(p, 127, 1) for p in part]
    out = []
    for b in range(n):
        before = left[b - 1] if b else 0.0
        after = right[b + 1] if b < n - 1 else 0.0
        out.append(
            part[b] + jnp.where(at == 0, before, left[b]) + jnp.where(at == 127, after, right[b])
        )
    return jnp.concatenate(out, axis=1)


class Geometry:
    def __init__(self, shape, ns, nl):
        self.nz, self.nx, self.NY = shape
        self.ns, self.nl = ns, nl
        self.NZ = self.nz * ns
        self.ny = self.NY // ns
        self.WY = min(self.NY, -(-(self.ny + 2 * YH) // 128) * 128)
        self.PW = -(-self.ny // 128) * 128
        self.nxm, self.nxl = self.nx // 2, self.nx // 4
        self.NZm, self.NZl = self.NZ // 2, self.NZ // 4
        self.WYm, self.NYm, self.NYl = self.WY // 2, self.NY // 2, self.NY // 4
        self.CH = max(1, min(4, 64 // self.NZ))
        self.PF = self.nx + 2 * OUT
        self.PM = self.nxm + 2 * MH
        self.PL = self.nxl + 2 * LH
        assert self.nx % self.CH == 0 and OUT % self.CH == 0 and XH <= self.nx
        assert self.nxl < LH <= 2 * self.nxl and MH <= self.nxm
        assert (self.nxl * self.nz // 4) % 4 == 0 and self.WYm % 128 == 0 and self.NYl % 128 == 0
        self.lowrows = self.nxl * (self.nz // 4)
        self.rows_1st = self.nz * self.nx + -(-3 * self.lowrows // 8) * 8
        self.rows_2nd = 2 * self.nz * self.nx

    def start(self, s):
        return jnp.clip(s * self.ny - (self.WY - self.ny) // 2, 0, self.NY - self.WY)


def vmem_call(kernel, outs, scratch, smem, args):
    specs = [pl.BlockSpec(memory_space=pltpu.SMEM)] * smem
    specs += [pl.BlockSpec(memory_space=pltpu.VMEM)] * (len(args) - smem)
    shapes = list(outs) + list(scratch) + [a.shape for a in args[smem:]]
    held = sum(4 * math.prod(o) for o in shapes)
    return pl.pallas_call(
        kernel,
        out_shape=[jax.ShapeDtypeStruct(o, F32) for o in outs],
        in_specs=specs,
        out_specs=[pl.BlockSpec(memory_space=pltpu.VMEM)] * len(outs),
        scratch_shapes=[pltpu.VMEM(o, F32) for o in scratch],
        compiler_params=pltpu.CompilerParams(vmem_limit_bytes=min(held * 3 // 2 + (4 << 20), 60 << 20)),
        interpret=INTERPRET,
    )(*args)


def repeat(g, n, body):
    if g.ns <= 4:
        for i in range(n):
            body(i)
    else:
        lax.fori_loop(0, n, lambda i, carry: (body(i), carry)[1], 0)


def pack_kernel(g, idx, near, *outs):
    s = idx[0]
    lane_pick = jnp.where(
        iota((g.NY, g.NYl), 0) // 4 == iota((g.NY, g.NYl), 1), 1.0, 0.0
    ).astype(F32)
    row_pick = jnp.where(
        iota((g.nxl, g.nx), 1) // 4 == iota((g.nxl, g.nx), 0), 1.0 / 64.0, 0.0
    ).astype(F32)
    base = g.nz * g.nx
    first, second = outs[: g.ns], outs[g.ns :]
    turns = []
    for k in range(g.ns):
        first[k][base:, :] = jnp.zeros((g.rows_1st - base, g.WY), F32)
        partner = lax.rem(s - k + g.ns, g.ns)
        turns.append(lax.rem(g.NY - g.start(partner), g.NY))
    for a, (group, at_a) in enumerate(((first, 0), (second, 0), (second, 1))):
        arr = near.at[a]
        for k in range(g.ns):

            def row(z, at_a=at_a, k=k, arr=arr, group=group):
                at = (at_a * g.nz + z) * g.nx
                if not isinstance(at, int):
                    at = pl.multiple_of(at, 8)
                v = pltpu.roll(arr[z], turns[k], 1)[:, : g.WY]
                group[k][pl.ds(at, g.nx), :] = v

            repeat(g, g.nz, row)
        for zl in range(g.nz // 4):
            col = arr[4 * zl] + arr[4 * zl + 1] + arr[4 * zl + 2] + arr[4 * zl + 3]
            low = dot(row_pick, dot(col, lane_pick))
            at = base + a * g.lowrows + zl * g.nxl
            for k in range(g.ns):
                first[k][at : at + g.nxl, : g.NYl] = low


def fine_to_mid(src, row, planes, nz, scale):
    n = planes * nz // 2
    lanes = src.shape[0] * 128
    v = blocks(src, pl.ds(row, n, stride=2)) + blocks(src, pl.ds(row + 1, n, stride=2))
    v = v.reshape(planes // 2, 2, nz // 2, lanes)
    v = (v[:, 0] + v[:, 1]).reshape(planes // 2 * (nz // 2), lanes)
    half = (lanes, lanes // 2)
    pick = jnp.where(iota(half, 0) // 2 == iota(half, 1), scale / 8.0, 0.0).astype(F32)
    return dot(v, pick)


def assemble_kernel(g, count, idx, *refs):
    s = idx[0]
    recv, refs = refs[: g.ns], refs[g.ns :]
    f_out, m_out, to_left, to_right = refs[:4]
    l_out, fs = refs[4] if count == 1 else None, refs[-1]
    base = count * g.nz * g.nx
    for j in range(g.ns):
        src = lax.rem(s + j, g.ns)
        for a in range(count):

            def row(z, a=a, j=j, src=src):
                at = (a * g.nz + z) * g.nx
                if not isinstance(at, int):
                    at = pl.multiple_of(at, 8)
                rows = pl.ds(src * g.nz + z, g.nx, stride=g.NZ)
                put_blocks(fs.at[a], rows, recv[j][pl.ds(at, g.nx), :])

            repeat(g, g.nz, row)
        for i in range(3 if count == 1 else 0):
            for zl in range(g.nz // 4):
                at = base + i * g.lowrows + zl * g.nxl
                for x in range(g.nxl):
                    l_out[i, pl.ds(x * g.NZl + src * (g.nz // 4) + zl, 1), :] = recv[j][
                        at + x : at + x + 1, : g.NYl
                    ]
    nxz = g.nx * g.NZ
    at, n = 0, XH * g.NZ
    for a in range(count):
        f_out[a] = blocks(fs.at[a], slice(0, nxz))
        m_out[a] = fine_to_mid(fs.at[a], 0, g.nx, g.NZ, 1.0)
        for b in range(g.WY // 128):
            to_left[at : at + n, :] = fs[a, b, 0:n, :]
            to_right[at : at + n, :] = fs[a, b, nxz - n :, :]
            at += n
    n, total = MH * g.NZm, g.nxm * g.NZm
    for a in range(count):
        for y in range(0, g.WYm, 128):
            to_left[at : at + n, :] = m_out[a, 0:n, y : y + 128]
            to_right[at : at + n, :] = m_out[a, total - n :, y : y + 128]
            at += n
    n = g.nxl * g.NZl
    for i in range(3 if count == 1 else 0):
        for y in range(0, g.NYl, 128):
            to_left[at : at + n, :] = l_out[i, :, y : y + 128]
            to_right[at : at + n, :] = l_out[i, :, y : y + 128]
            at += n


def edge_rows(g, count):
    rows = count * XH * g.NZ * (g.WY // 128) + count * MH * g.NZm * (g.WYm // 128)
    return rows + (3 * g.nxl * g.NZl * (g.NYl // 128) if count == 1 else 0)


def coefficients(b, c, q):
    diag = c * c + q
    inv = 1.0 / diag
    scaled = (27.0 / 26.0 * (c * c) + q) * inv
    return diag, inv, scaled, c * inv / 26.0


def coarse_smooth(g, idx, tab, mid, low):
    for level, (gi, c, D, K, y, d, t) in ((1, mid), (2, low)):
        y[...] = gi[...] * tab[level, 0]
        d[...] = y[...]

    def turn(j, carry):
        for nz, (gi, c, D, K, y, d, t) in ((g.NZm, mid), (g.NZl, low)):
            rows = c.shape[0]
            t[nz : nz + rows, :] = zy_sum(c[...] * y[...], nz)
        for level, nz, (gi, c, D, K, y, d, t) in ((1, g.NZm, mid), (2, g.NZl, low)):
            rows = c.shape[0]
            box = t[0:rows, :] + t[nz : nz + rows, :] + t[2 * nz : 2 * nz + rows, :]
            e = gi[...] - D[...] * y[...] + K[...] * box
            nd = tab[level, j] * d[...] + tab[level, MAXDEG + j] * e
            d[...] = nd
            y[...] = y[...] + nd
        return carry

    lax.fori_loop(1, jnp.maximum(idx[3], idx[4]), turn, 0)


def fine_sweeps(g, idx, tab, gi, c, D, K, y, d):
    nz = g.NZ

    def rows(p):
        return slice((OUT + p) * nz, (OUT + p + 1) * nz)

    for p in range(-XH, g.nx + XH):
        r = rows(p)
        y[r, :] = gi[r, :] * tab[0, 0]
        d[r, :] = y[r, :]
    for j in range(1, MAXDEG):
        reach = MAXDEG - j

        @pl.when(j < idx[2])
        def _(j=j, reach=reach):
            alpha, beta = tab[0, j], tab[0, MAXDEG + j]
            first, last = -reach - 1, g.nx + reach
            held, sums = {}, {}
            for p in range(first, last + 1):
                held[p] = y[rows(p), :]
                sums[p] = zy_sum(c[rows(p), :] * held[p], nz)
                q = p - 1
                if q <= first:
                    continue
                r = rows(q)
                box = sums[q - 1] + sums[q] + sums[p]
                e = gi[r, :] - D[r, :] * held[q] + K[r, :] * box
                nd = alpha * d[r, :] + beta * e
                d[r, :] = nd
                y[r, :] = held[q] + nd


def fine_smooth(g, idx, tab, gi, c, D, K, y, d, t):
    if g.NZ <= 16:
        fine_sweeps(g, idx, tab, gi, c, D, K, y, d)
        return
    n = g.CH * g.NZ
    side, own = OUT // g.CH, g.nx // g.CH
    y[...] = gi[...] * tab[0, 0]
    d[...] = y[...]

    def turn(j, carry):
        radius = idx[2] - j
        ht = (radius + 1 + g.CH - 1) // g.CH
        h = (radius + g.CH - 1) // g.CH
        fine_boxes(g, side - ht, side + own + ht, c, y, t)

        def chunk(k, inner_carry):
            r = pl.ds(pl.multiple_of(k * n, n), n)
            old = y[r, :]
            e = gi[r, :] - D[r, :] * old + K[r, :] * box_at(g, t, k)
            nd = tab[0, j] * d[r, :] + tab[0, MAXDEG + j] * e
            d[r, :] = nd
            y[r, :] = old + nd
            return inner_carry

        lax.fori_loop(side - h, side + own + h, chunk, 0)
        return carry

    lax.fori_loop(1, idx[2], turn, 0)


def clear_box_edges(g, t, tm, tl):
    for ref, nz in ((t, g.NZ), (tm, g.NZm), (tl, g.NZl)):
        zeros = jnp.zeros((nz, ref.shape[1]), F32)
        ref[0:nz, :] = zeros
        ref[ref.shape[0] - nz :, :] = zeros


def fine_boxes(g, first, last, c, x, t):
    n = g.CH * g.NZ

    def turn(k, carry):
        r = pl.ds(pl.multiple_of(k * n, n), n)
        t[pl.ds(pl.multiple_of(g.NZ + k * n, g.NZ), n), :] = zy_sum(c[r, :] * x[r, :], g.NZ)
        return carry

    lax.fori_loop(first, last, turn, 0)


def box_at(g, t, k):
    n = g.CH * g.NZ
    parts = [t[pl.ds(pl.multiple_of(k * n + o * g.NZ, g.NZ), n), :] for o in range(3)]
    return parts[0] + parts[1] + parts[2]


def coarse_correction(g, s, ym, yl, zd):
    planes = g.nxm + 2
    rows = planes * g.NZm
    shape = (rows, g.PL * g.NZl)
    row, col = iota(shape, 0), iota(shape, 1)
    plane = row // g.NZm + (2 * LH - 1)
    want = (plane // 2) * g.NZl + (row % g.NZm) // 2
    up_rows = jnp.where(col == want, 1.0, 0.0).astype(F32)
    shape = (g.NYl, g.WYm)
    off = g.start(s) // 4
    up_lanes = jnp.where(
        iota(shape, 0) == off + iota(shape, 1) // 2, 1.0, 0.0
    ).astype(F32)
    low = dot(dot(up_rows, yl[...]), up_lanes)
    at = (MH - 1) * g.NZm
    both = ym[at : at + rows, :] + low
    shape = (g.WYm, g.WY)
    wide = jnp.where(iota(shape, 0) == iota(shape, 1) // 2, 1.0, 0.0).astype(F32)
    v = dot(both, wide)
    put_blocks(zd, pl.ds(0, rows, stride=2), v)
    put_blocks(zd, pl.ds(1, rows, stride=2), v)


def doubled(g, zd, plane, planes):
    at = (plane + 2) // 2 * g.NZ
    if planes == 1:
        return blocks(zd, slice(at, at + g.NZ))
    v = blocks(zd, slice(at, at + planes // 2 * g.NZ)).reshape(planes // 2, 1, g.NZ, g.WY)
    v = jnp.broadcast_to(v, (planes // 2, 2, g.NZ, g.WY))
    return v.reshape(planes * g.NZ, g.WY)


def pieces(g):
    return [(-1, 1)] + [(p, g.CH) for p in range(0, g.nx, g.CH)] + [(g.nx, 1)]


def cycle(g, idx, tab, fine, mid, low, x_old, x, bi, diag, zd, keep, xb=None):
    _, c, D, K, y, _, t = fine
    fine_smooth(g, idx, tab, *fine)
    coarse_smooth(g, idx, tab, mid, low)
    coarse_correction(g, idx[0], mid[4], low[4], zd)
    for p, planes in pieces(g):
        n = planes * g.NZ
        rr = slice((OUT + p) * g.NZ, (OUT + p) * g.NZ + n)
        r = slice((1 + p) * g.NZ, (1 + p) * g.NZ + n)
        v = 0.5 * (y[rr, :] + doubled(g, zd, p, planes))
        if x_old is not None:
            v = x_old[r, :] + v
        x[r, :] = v
        if xb is not None and planes == g.CH and 0 <= p < g.nx:
            put_blocks(xb, slice(p * g.NZ, p * g.NZ + n), v)
        t[r, :] = zy_sum(c[rr, :] * v, g.NZ)
    step = g.CH * g.NZ
    for p in range(0, g.nx, g.CH):
        at = p * g.NZ
        box = (
            t[at : at + step, :]
            + t[at + g.NZ : at + g.NZ + step, :]
            + t[at + 2 * g.NZ : at + 2 * g.NZ + step, :]
        )
        r = slice(at, at + step)
        rr = slice(OUT * g.NZ + at, OUT * g.NZ + at + step)
        v = bi[r, :] - D[rr, :] * x[at + g.NZ : at + g.NZ + step, :] + K[rr, :] * box
        keep(r, v, v * diag[r, :])


def send_defect(g, s, gi, rm, rl, res, to_l, to_r, to_l2, to_r2):
    rm[...] = fine_to_mid(res, 0, g.nx, g.NZ, 4.0)
    shape = (g.nxl * g.NZl, g.nxm * g.NZm)
    row, col = iota(shape, 0), iota(shape, 1)
    same_x = col // (2 * g.NZm) == row // g.NZl
    same_z = (col % g.NZm) // 2 == row % g.NZl
    rows = jnp.where(same_x & same_z, 0.5, 0.0).astype(F32)
    shape = (g.WYm, g.NYl)
    off = g.start(s) // 4
    lanes = jnp.where(iota(shape, 0) // 2 + off == iota(shape, 1), 1.0, 0.0).astype(F32)
    rl[...] = dot(dot(rows, rm[...]), lanes)
    at = 0
    for ref, n in ((gi, XH * g.NZ), (rm, MH * g.NZm), (rl, g.nxl * g.NZl)):
        total = ref.shape[0]
        for y in range(0, ref.shape[1], 128):
            to_l[at : at + n, :] = ref[0:n, y : y + 128]
            to_r[at : at + n, :] = ref[total - n :, y : y + 128]
            at += n
    far = (LH - g.nxl) * g.NZl
    total = rl.shape[0]
    for b in range(g.NYl // 128):
        lanes = slice(128 * b, 128 * b + 128)
        to_l2[b * far : b * far + far, :] = rl[0:far, lanes]
        to_r2[b * far : b * far + far, :] = rl[total - far :, lanes]


def first_kernel(g, idx, tab, *refs):
    f, m, l, f2nd, m2nd, from_l, from_r, from_l2nd, from_r2nd, from_l2, from_r2 = refs[:11]
    refs = refs[11:]
    (c, D, K, bi, diag, cm, Dm, Km, im, cl, Dl, Kl, il) = refs[:13]
    x, gi_own, rm, rl, to_l, to_r, to_l2, to_r2 = refs[13:21]
    (gi, y, d, t, gm, ym, dm, tm, gl, yl, dl, tl, zd, res) = refs[21:]
    s, li = idx[0], idx[1]
    clear_box_edges(g, t, tm, tl)
    fill = (0.0, 0.0, 1.0)

    def kept(ok, v, a):
        return jnp.where(ok, v, fill[a])

    n = XH * g.NZ
    lo, hi = OUT * g.NZ, (OUT + g.nx) * g.NZ
    at = {0: 0, 1: 0}
    region = (gi, c, y)
    for a in range(3):
        left, right = (from_l2nd, from_r2nd) if a else (from_l, from_r)
        q = min(a, 1)
        region[a][0 : lo - n, :] = jnp.full((lo - n, g.WY), fill[a], F32)
        region[a][hi + n :, :] = jnp.full((lo - n, g.WY), fill[a], F32)
        region[a][lo:hi, :] = f2nd[a - 1] if a else f[0]
        for yy in range(0, g.WY, 128):
            rows = slice(at[q], at[q] + n)
            region[a][lo - n : lo, yy : yy + 128] = kept(li > 0, left[rows, :], a)
            region[a][hi : hi + n, yy : yy + 128] = kept(
                li < g.nl - 1, right[rows, :], a
            )
            at[q] += n
    step = g.CH * g.NZ

    def build(k, carry):
        r = pl.ds(pl.multiple_of(k * step, step), step)
        b0 = gi[r, :]
        dg, inv, sc, kk = coefficients(b0, c[r, :], y[r, :])
        gi[r, :] = b0 * inv
        D[r, :] = sc
        K[r, :] = kk
        y[r, :] = dg
        return carry

    lax.fori_loop(0, g.PF // g.CH, build, 0)
    bi[...] = gi[lo:hi, :]
    diag[...] = y[lo:hi, :]

    n = MH * g.NZm
    parts = []
    for a in range(3):
        halves = []
        left, right = (from_l2nd, from_r2nd) if a else (from_l, from_r)
        q = min(a, 1)
        for _ in range(0, g.WYm, 128):
            rows = slice(at[q], at[q] + n)
            halves.append(
                (kept(li > 0, left[rows, :], a), kept(li < g.nl - 1, right[rows, :], a))
            )
            at[q] += n
        left = jnp.concatenate([v[0] for v in halves], axis=1)
        right = jnp.concatenate([v[1] for v in halves], axis=1)
        own_mid = m2nd[a - 1] if a else m[0]
        parts.append(jnp.concatenate([left, own_mid, right], axis=0))
    _, inv, sc, kk = coefficients(*parts)
    cm[...] = parts[1]
    Dm[...] = sc
    Km[...] = kk
    im[...] = inv
    gm[...] = 4.0 * parts[0] * inv

    n = g.nxl * g.NZl
    far = (LH - g.nxl) * g.NZl
    store = (gl, cl, il)
    at, at2 = at[0], 0
    for a in range(3):
        for yy in range(0, g.NYl, 128):
            lanes = slice(yy, yy + 128)
            ref = store[a]
            ref[0:far, lanes] = kept(li > 1, from_l2[at2 : at2 + far, :], a)
            ref[far : far + n, lanes] = kept(li > 0, from_l[at : at + n, :], a)
            ref[far + n : far + 2 * n, lanes] = l[a, :, lanes]
            ref[far + 2 * n : far + 3 * n, lanes] = kept(
                li < g.nl - 1, from_r[at : at + n, :], a
            )
            ref[far + 3 * n :, lanes] = kept(li < g.nl - 2, from_r2[at2 : at2 + far, :], a)
            at += n
            at2 += far
    _, inv, sc, kk = coefficients(gl[...], cl[...], il[...])
    Dl[...] = sc
    Kl[...] = kk
    il[...] = inv
    gl[...] = 16.0 * gl[...] * inv

    def keep(r, scaled, plain):
        gi_own[r, :] = scaled
        put_blocks(res, r, plain)

    fine = (gi, c, D, K, y, d, t)
    mid = (gm, cm, Dm, Km, ym, dm, tm)
    low = (gl, cl, Dl, Kl, yl, dl, tl)
    cycle(g, idx, tab, fine, mid, low, None, x, bi, diag, zd, keep)
    send_defect(g, s, gi_own, rm, rl, res, to_l, to_r, to_l2, to_r2)


def gather_defect(g, gi_own, rm, rl, from_l, from_r, from_l2, from_r2, gi, gm, im, gl, il):
    lo, hi = OUT * g.NZ, (OUT + g.nx) * g.NZ
    n = XH * g.NZ
    zeros = jnp.zeros((lo - n, g.WY), F32)
    gi[0 : lo - n, :] = zeros
    gi[hi + n :, :] = zeros
    gi[lo:hi, :] = gi_own[...]
    at = 0
    for y in range(0, g.WY, 128):
        gi[lo - n : lo, y : y + 128] = from_l[at : at + n, :]
        gi[hi : hi + n, y : y + 128] = from_r[at : at + n, :]
        at += n
    n, own = MH * g.NZm, rm.shape[0]
    for y in range(0, g.WYm, 128):
        lanes = slice(y, y + 128)
        gm[0:n, lanes] = from_l[at : at + n, :] * im[0:n, lanes]
        gm[n + own :, lanes] = from_r[at : at + n, :] * im[n + own :, lanes]
        at += n
    gm[n : n + own, :] = rm[...] * im[n : n + own, :]
    n = g.nxl * g.NZl
    far = (LH - g.nxl) * g.NZl
    for b in range(g.NYl // 128):
        lanes = slice(128 * b, 128 * b + 128)
        rows = slice(b * far, b * far + far)
        gl[0:far, lanes] = from_l2[rows, :]
        gl[far : far + n, lanes] = from_l[at : at + n, :]
        gl[far + n : far + 2 * n, lanes] = rl[:, lanes]
        gl[far + 2 * n : far + 3 * n, lanes] = from_r[at : at + n, :]
        gl[far + 3 * n :, lanes] = from_r2[rows, :]
        at += n
    gl[...] = gl[...] * il[...]


def cycle_kernel(g, n_outs, idx, tab, *refs):
    gi_own, rm, rl, x_old = refs[:4]
    received = refs[4:8]
    (c, D, K, bi, diag, cm, Dm, Km, im, cl, Dl, Kl, il) = refs[8:21]
    outs = refs[21 : 21 + n_outs]
    scr = refs[21 + n_outs :]
    (gi, y, d, t, gm, ym, dm, tm, gl, yl, dl, tl, zd, res) = scr[:14]
    clear_box_edges(g, t, tm, tl)
    gather_defect(g, gi_own, rm, rl, *received, gi, gm, im, gl, il)
    fine = (gi, c, D, K, y, d, t)
    mid = (gm, cm, Dm, Km, ym, dm, tm)
    low = (gl, cl, Dl, Kl, yl, dl, tl)
    s = idx[0]
    if len(scr) == 14:
        x, gi_new, rm_new, rl_new = outs[:4]

        def keep(r, scaled, plain):
            gi_new[r, :] = scaled
            put_blocks(res, r, plain)

        cycle(g, idx, tab, fine, mid, low, x_old, x, bi, diag, zd, keep)
        send_defect(g, s, gi_new, rm_new, rl_new, res, *outs[4:])
        return
    x, xb = scr[14:]

    def keep_plain(r, scaled, plain):
        put_blocks(res, r, plain)

    cycle(g, idx, tab, fine, mid, low, x_old, x, bi, diag, zd, keep_plain, xb)
    shift = lax.rem(g.WY - (s * g.ny - g.start(s)), g.WY)
    for k in range(g.ns):
        partner = lax.rem(s - k + g.ns, g.ns)
        for o, ref in enumerate((xb, res)):

            def row(z, o=o, ref=ref, k=k, partner=partner):
                v = blocks(ref, pl.ds(partner * g.nz + z, g.nx, stride=g.NZ))
                at = (o * g.nz + z) * g.nx
                if not isinstance(at, int):
                    at = pl.multiple_of(at, 8)
                outs[k][pl.ds(at, g.nx), :] = pltpu.roll(v, shift, 1)[:, : g.PW]

            repeat(g, g.nz, row)


def unpack_kernel(g, idx, *refs):
    s = idx[0]
    recv, outs = refs[: g.ns], refs[g.ns :]
    for o in range(2):
        for z in range(g.nz):
            at = (o * g.nz + z) * g.nx
            total = None
            if g.ny % 128 == 0:
                wide = jnp.concatenate(
                    [recv[j][at : at + g.nx, : g.ny] for j in range(g.ns)], axis=1
                )
                total = pltpu.roll(wide, s * g.ny, 1)
            else:
                mine = iota((g.nx, g.NY), 1) < g.ny
                for j in range(g.ns):
                    src = lax.rem(s + j, g.ns)
                    v = recv[j][at : at + g.nx, :]
                    pad = jnp.zeros((g.nx, g.NY - g.PW), F32)
                    v = jnp.where(mine, jnp.concatenate([v, pad], axis=1), 0.0)
                    v = pltpu.roll(v, src * g.ny, 1)
                    total = v if total is None else total + v
            outs[o][z] = total


def ring(value, axis, by):
    peers = lax.axis_size(axis)
    if by % peers == 0:
        return value
    return lax.ppermute(value, axis, [(i, (i - by) % peers) for i in range(peers)])


def sweep_tables(degrees, lower, upper):
    centre = (upper + lower) * 0.5
    radius = (upper - lower) * 0.5
    ratio = centre / radius
    rho = 1.0 / ratio
    alphas, betas = [], []
    for j in range(1, MAXDEG):
        new = 1.0 / (2.0 * ratio - rho)
        active = j < degrees
        alphas.append(jnp.where(active, new * rho, 0.0))
        betas.append(jnp.where(active, 2.0 * new / radius, 0.0))
        rho = new
    zero = jnp.zeros_like(rho)
    return jnp.stack([1.0 / centre] + alphas + [zero] + betas, axis=1)


def shards(right_side, scale_field, mass_field, degrees, lower_bound, upper_bound):
    g = Geometry(right_side.shape, lax.axis_size("slab"), lax.axis_size("level"))
    place = jnp.stack([lax.axis_index("slab"), lax.axis_index("level")])
    place = place.astype(jnp.int32)
    idx = jnp.concatenate([place, degrees])
    tab = sweep_tables(degrees, lower_bound, upper_bound)

    def call(kernel, outs, scratch, smem, *args):
        return vmem_call(lambda *refs: kernel(g, *refs), outs, scratch, smem, args)

    shape = right_side.shape
    packs = call(
        pack_kernel, [(g.rows_1st, g.WY)] * g.ns + [(g.rows_2nd, g.WY)] * g.ns, [], 1,
        place, jnp.stack([right_side, scale_field, mass_field]),
    )
    packs_1st, packs_2nd = [], []
    for k in range(g.ns):
        packs_1st.append(ring(packs[k], "slab", k))
    for k in range(g.ns):
        packs_2nd.append(ring(packs[g.ns + k], "slab", k))

    fine = (g.PF * g.NZ, g.WY)
    own = (g.nx * g.NZ, g.WY)
    mid = (g.PM * g.NZm, g.WYm)
    low = (g.PL * g.NZl, g.NYl)
    own_blocks = (g.WY // 128, own[0], 128)
    scratch = [
        fine, fine, fine, (fine[0] + 2 * g.NZ, g.WY),
        mid, mid, mid, (mid[0] + 2 * g.NZm, g.WYm),
        low, low, low, (low[0] + 2 * g.NZl, g.NYl),
        (g.WY // 128, (g.nxm + 2) * g.NZ, 128), own_blocks,
    ]

    def assemble(count, packs):
        outs = [
            (count, *own), (count, g.nxm * g.NZm, g.WYm),
            (edge_rows(g, count), 128), (edge_rows(g, count), 128),
        ] + [(3, g.nxl * g.NZl, g.NYl)] * (count == 1)
        return vmem_call(
            lambda *refs: assemble_kernel(g, count, *refs),
            outs, [(count, *own_blocks)], 1, (place, *packs),
        )

    f, m, to_left, to_right, l = assemble(1, packs_1st)
    far = (LH - g.nxl) * g.NZl
    lanes = g.NYl // 128

    def far_rows(part):
        parts = part.reshape(3, part.shape[1], lanes, 128)
        return parts.transpose(0, 2, 1, 3).reshape(3 * lanes * far, 128)

    from_l = ring(to_right, "level", -1)
    from_r = ring(to_left, "level", 1)
    from_l2 = ring(far_rows(l[:, l.shape[1] - far :]), "level", -2)
    from_r2 = ring(far_rows(l[:, :far]), "level", 2)

    f2nd, m2nd, to_left, to_right = assemble(2, packs_2nd)
    from_l2nd = ring(to_right, "level", -1)
    from_r2nd = ring(to_left, "level", 1)

    x_shape = ((g.nx + 2) * g.NZ, g.WY)
    rm_shape, rl_shape = (g.nxm * g.NZm, g.WYm), (g.nxl * g.NZl, g.NYl)
    sent = (
        XH * g.NZ * (g.WY // 128) + MH * g.NZm * (g.WYm // 128) + rl_shape[0] * lanes,
        128,
    )
    sent2 = (lanes * far, 128)
    state = [x_shape, own, rm_shape, rl_shape, sent, sent, sent2, sent2]
    outs = call(
        first_kernel, [fine] * 3 + [own] * 2 + [mid] * 4 + [low] * 4 + state, scratch, 2,
        idx, tab, f, m, l, f2nd, m2nd,
        from_l, from_r, from_l2nd, from_r2nd, from_l2, from_r2,
    )
    coefs, outs = outs[:13], outs[13:]
    for cycle_no in range(1, CYCLES):
        x, gi, rm, rl, to_l, to_r, to_l2, to_r2 = outs
        received = (
            ring(to_r, "level", -1),
            ring(to_l, "level", 1),
            ring(to_r2, "level", -2),
            ring(to_l2, "level", 2),
        )
        if cycle_no < CYCLES - 1:
            shapes, more = state, []
        else:
            shapes, more = [(2 * g.nz * g.nx, g.PW)] * g.ns, [x_shape, own_blocks]
        outs = vmem_call(
            lambda *refs, n=len(shapes): cycle_kernel(g, n, *refs),
            shapes, scratch + more, 2,
            (idx, tab, gi, rm, rl, x, *received, *coefs),
        )
    packs = [ring(v, "slab", k) for k, v in enumerate(outs)]
    return tuple(call(unpack_kernel, [shape, shape], [], 1, place, *packs))


def solution(mesh):
    spread = P("slab", "level", None)
    return jax.shard_map(
        shards,
        mesh=mesh,
        in_specs=(spread, spread, spread, P(), P(), P()),
        out_specs=(spread, spread),
        check_vma=False,
    )
```

profile of v0, /device:TPU:0, one launch (start us, length us, event | category | flops | bytes accessed | tf_op | source)
XLA Modules:
  0.0 77.3 jit_solution(14486767006492136078)
XLA Ops:
  1.8 1.5 %shard_map.77 = (f32[80,256]{1,0:T(8,128)S(1)}, f32[80,256]{1,0:T(8,128)S(1)}, f32[80,256]{1,0:T(8,128)S(1)}, f32[80,256]{1,0:T(8,128)S(1)}, f32[128,256]{1,0:T(...) custom-call(s32[2]{0:T(128)S(1)} %pad_add_fusion.refs_0_, ...), custom_call_target="tpu_custom_call" | custom-call | tf_op jit(solution)/shard_map/pallas_call | solution.py:105
  3.2 5.1 %collective-permute-start = (f32[80,256]{1,0:T(8,128)S(1)}, f32[80,256]{1,0:T(8,128)S(1)}, u32[]{:S(2)}, u32[]{:S(2)}) collective-permute-start(f32[80,256]{1,0:T(8,128)S(1)} %get-tuple-element.53), channel_id=1, source_target_pairs={{0,3},{1,0},{2,1},{3,2},{4,7},{5,4},{6,5},{7,6},{8,11},{9,8},{10,9... | collective-permute-start | bytes 245768 | tf_op jit(solution)/shard_map/ppermute | solution.py:637
  9.3 2.8 %collective-permute-start.3 = (f32[128,256]{1,0:T(8,128)S(1)}, f32[128,256]{1,0:T(8,128)S(1)}, u32[]{:S(2)}, u32[]{:S(2)}) collective-permute-start(f32[128,256]{1,0:T(8,128)S(1)} %get-tuple-element.60), channel_id=1, source_target_pairs={{0,3},{1,0},{2,1},{3,2},{4,7},{5,4},{6,5},{7,6},{8,11},{9,8},{10,9... | collective-permute-start | bytes 393224 | tf_op jit(solution)/shard_map/ppermute | solution.py:637
  12.1 1.1 %collective-permute-start.4 = (f32[128,256]{1,0:T(8,128)S(1)}, f32[128,256]{1,0:T(8,128)S(1)}, u32[]{:S(2)}, u32[]{:S(2)}) collective-permute-start(f32[128,256]{1,0:T(8,128)S(1)} %get-tuple-element.61), channel_id=1, source_target_pairs={{0,2},{1,3},{2,0},{3,1},{4,6},{5,7},{6,4},{7,5},{8,10},{9,11},{10,... | collective-permute-start | bytes 393224 | tf_op jit(solution)/shard_map/ppermute | solution.py:637
  14.0 2.2 %collective-permute-done.1.refs_3_ = f32[80,256]{1,0:T(8,128)S(1)} collective-permute-done((f32[80,256]{1,0:T(8,128)S(1)}, f32[80,256]{1,0:T(8,128)S(1)}, u32[]{:S(2)}, u32[]{:S(2)}) %collective-permute-start.1) | collective-permute-done | bytes 81952 | tf_op jit(solution)/shard_map/ppermute | solution.py:637
  17.1 2.5 %collective-permute-start.11 = (f32[24,128]{1,0:T(8,128)S(1)}, f32[24,128]{1,0:T(8,128)S(1)}, u32[]{:S(2)}, u32[]{:S(2)}) collective-permute-start(f32[24,128]{1,0:T(8,128)S(1)} %get-tuple-element.111), channel_id=1, source_target_pairs={{0,24},{4,28},{8,0},{12,4},{16,8},{20,12},{24,16},{28,20},{1,25},{... | collective-permute-start | bytes 36872 | tf_op jit(solution)/shard_map/ppermute | solution.py:637
  19.6 2.6 %collective-permute-start.7 = (f32[288,128]{1,0:T(8,128)S(1)}, f32[288,128]{1,0:T(8,128)S(1)}, u32[]{:S(2)}, u32[]{:S(2)}) collective-permute-start(f32[288,128]{1,0:T(8,128)S(1)} %get-tuple-element.66), channel_id=1, source_target_pairs={{0,28},{4,0},{8,4},{12,8},{16,12},{20,16},{24,20},{28,24},{1,29},{... | collective-permute-start | bytes 442376 | tf_op jit(solution)/shard_map/ppermute | solution.py:637
  22.3 4.8 %collective-permute-done.4.refs_3_ = f32[128,256]{1,0:T(8,128)S(1)} collective-permute-done((f32[128,256]{1,0:T(8,128)S(1)}, f32[128,256]{1,0:T(8,128)S(1)}, u32[]{:S(2)}, u32[]{:S(2)}) %collective-permute-start.4) | collective-permute-done | bytes 131104 | tf_op jit(solution)/shard_map/ppermute | solution.py:637
  28.2 2.6 %collective-permute-start.9 = (f32[480,128]{1,0:T(8,128)S(1)}, f32[480,128]{1,0:T(8,128)S(1)}, u32[]{:S(2)}, u32[]{:S(2)}) collective-permute-start(f32[480,128]{1,0:T(8,128)S(1)} %get-tuple-element.68), channel_id=1, source_target_pairs={{0,28},{4,0},{8,4},{12,8},{16,12},{20,16},{24,20},{28,24},{1,29},{... | collective-permute-start | bytes 737288 | tf_op jit(solution)/shard_map/ppermute | solution.py:637
  32.7 4.9 %collective-permute-done.10.refs_11_ = f32[24,128]{1,0:T(8,128)S(1)} collective-permute-done((f32[24,128]{1,0:T(8,128)S(1)}, f32[24,128]{1,0:T(8,128)S(1)}, u32[]{:S(2)}, u32[]{:S(2)}) %collective-permute-start.10) | collective-permute-done | bytes 12320 | tf_op jit(solution)/shard_map/ppermute | solution.py:637
  37.7 5.0 %shard_map.80 = (f32[512,256]{1,0:T(8,128)S(1)}, f32[512,256]{1,0:T(8,128)S(1)}, f32[512,256]{1,0:T(8,128)S(1)}, f32[256,256]{1,0:T(8,128)S(1)}, f32[256,256]{1,...) custom-call(s32[5]{0:T(128)S(1)} %pad_add_fusion.1.refs_0_, ...), custom_call_target="tpu_custom_call" | custom-call | tf_op jit(solution)/shard_map/pallas_call | solution.py:105
  42.7 2.7 %collective-permute-start.13 = (f32[256,128]{1,0:T(8,128)S(1)}, f32[256,128]{1,0:T(8,128)S(1)}, u32[]{:S(2)}, u32[]{:S(2)}) collective-permute-start(f32[256,128]{1,0:T(8,128)S(1)} %get-tuple-element.74), channel_id=1, source_target_pairs={{0,28},{4,0},{8,4},{12,8},{16,12},{20,16},{24,20},{28,24},{1,29},{... | collective-permute-start | bytes 393224 | tf_op jit(solution)/shard_map/ppermute | solution.py:637
  45.4 2.9 %collective-permute-start.15 = (f32[8,128]{1,0:T(8,128)S(1)}, f32[8,128]{1,0:T(8,128)S(1)}, u32[]{:S(2)}, u32[]{:S(2)}) collective-permute-start(f32[8,128]{1,0:T(8,128)S(1)} %get-tuple-element.76), channel_id=1, source_target_pairs={{0,24},{4,28},{8,0},{12,4},{16,8},{20,12},{24,16},{28,20},{1,25},{... | collective-permute-start | bytes 12296 | tf_op jit(solution)/shard_map/ppermute | solution.py:637
  48.3 1.6 %collective-permute-done.14.refs_8_ = f32[8,128]{1,0:T(8,128)S(1)} collective-permute-done((f32[8,128]{1,0:T(8,128)S(1)}, f32[8,128]{1,0:T(8,128)S(1)}, u32[]{:S(2)}, u32[]{:S(2)}) %collective-permute-start.14) | collective-permute-done | bytes 4128 | tf_op jit(solution)/shard_map/ppermute | solution.py:637
  50.0 4.6 %shard_map.81 = (f32[288,256]{1,0:T(8,128)S(1)}, f32[256,256]{1,0:T(8,128)S(1)}, f32[64,128]{1,0:T(8,128)S(1)}, f32[16,128]{1,0:T(8,128)S(1)}, f32[256,128]{1,0:...) custom-call(s32[5]{0:T(128)S(1)} %pad_add_fusion.1.refs_0_, ...), custom_call_target="tpu_custom_call" | custom-call | tf_op jit(solution)/shard_map/pallas_call | solution.py:105
  54.6 2.7 %collective-permute-start.17 = (f32[256,128]{1,0:T(8,128)S(1)}, f32[256,128]{1,0:T(8,128)S(1)}, u32[]{:S(2)}, u32[]{:S(2)}) collective-permute-start(f32[256,128]{1,0:T(8,128)S(1)} %get-tuple-element.95), channel_id=1, source_target_pairs={{0,28},{4,0},{8,4},{12,8},{16,12},{20,16},{24,20},{28,24},{1,29},{... | collective-permute-start | bytes 393224 | tf_op jit(solution)/shard_map/ppermute | solution.py:637
  57.2 2.0 %collective-permute-start.18 = (f32[8,128]{1,0:T(8,128)S(1)}, f32[8,128]{1,0:T(8,128)S(1)}, u32[]{:S(2)}, u32[]{:S(2)}) collective-permute-start(f32[8,128]{1,0:T(8,128)S(1)} %get-tuple-element.96), channel_id=1, source_target_pairs={{0,8},{4,12},{8,16},{12,20},{16,24},{20,28},{24,0},{28,4},{1,9},{5... | collective-permute-start | bytes 12296 | tf_op jit(solution)/shard_map/ppermute | solution.py:637
  60.1 2.1 %collective-permute-done.18.refs_8_ = f32[8,128]{1,0:T(8,128)S(1)} collective-permute-done((f32[8,128]{1,0:T(8,128)S(1)}, f32[8,128]{1,0:T(8,128)S(1)}, u32[]{:S(2)}, u32[]{:S(2)}) %collective-permute-start.18) | collective-permute-done | bytes 4128 | tf_op jit(solution)/shard_map/ppermute | solution.py:637
  62.8 4.3 %shard_map.82 = (f32[128,128]{1,0:T(8,128)S(1)}, f32[128,128]{1,0:T(8,128)S(1)}, f32[128,128]{1,0:T(8,128)S(1)}, f32[128,128]{1,0:T(8,128)S(1)}) custom-call(s32[5]{0:T(128)S(1)} %pad_add_fusion.1.refs_0_, f32[3,12]{1,0:T(4,128)S(1)} %stack.71.refs_1_, f32[256,256]{1,0:T(8,128)S(1)} %get-tuple-element.90.refs_2_, f32[64,128]{1,0:T(8,128)S(1)} %get-tuple-element.91.refs_3_, ...), custom_call_target="tpu_custom_call" | custom-call | tf_op jit(solution)/shard_map/pallas_call | solution.py:105
  68.1 1.8 %collective-permute-start.21 = (f32[128,128]{1,0:T(8,128)S(1)}, f32[128,128]{1,0:T(8,128)S(1)}, u32[]{:S(2)}, u32[]{:S(2)}) collective-permute-start(f32[128,128]{1,0:T(8,128)S(1)} %get-tuple-element.100), channel_id=1, source_target_pairs={{0,2},{1,3},{2,0},{3,1},{4,6},{5,7},{6,4},{7,5},{8,10},{9,11},{10,... | collective-permute-start | bytes 196616 | tf_op jit(solution)/shard_map/ppermute | solution.py:637
  69.9 1.9 %collective-permute-start.22 = (f32[128,128]{1,0:T(8,128)S(1)}, f32[128,128]{1,0:T(8,128)S(1)}, u32[]{:S(2)}, u32[]{:S(2)}) collective-permute-start(f32[128,128]{1,0:T(8,128)S(1)} %get-tuple-element.101), channel_id=1, source_target_pairs={{0,1},{1,2},{2,3},{3,0},{4,5},{5,6},{6,7},{7,4},{8,9},{9,10},{10,1... | collective-permute-start | bytes 196616 | tf_op jit(solution)/shard_map/ppermute | solution.py:637
  71.9 2.1 %collective-permute-done.21.refs_3_ = f32[128,128]{1,0:T(8,128)S(1)} collective-permute-done((f32[128,128]{1,0:T(8,128)S(1)}, f32[128,128]{1,0:T(8,128)S(1)}, u32[]{:S(2)}, u32[]{:S(2)}) %collective-permute-start.21) | collective-permute-done | bytes 65568 | tf_op jit(solution)/shard_map/ppermute | solution.py:637
  74.0 1.9 %collective-permute-done.22.refs_4_ = f32[128,128]{1,0:T(8,128)S(1)} collective-permute-done((f32[128,128]{1,0:T(8,128)S(1)}, f32[128,128]{1,0:T(8,128)S(1)}, u32[]{:S(2)}, u32[]{:S(2)}) %collective-permute-start.22) | collective-permute-done | bytes 65568 | tf_op jit(solution)/shard_map/ppermute | solution.py:637
  75.9 1.3 %shard_map.83 = (f32[4,16,512]{2,1,0:T(8,128)}, f32[4,16,512]{2,1,0:T(8,128)}) custom-call(s32[2]{0:T(128)S(1)} %pad_add_fusion.refs_0_, f32[128,128]{1,0:T(8,128)S(1)} %get-tuple-element.98.refs_1_, f32[128,128]{1,0:T(8,128)S(1)} %collective-permute-done.20.refs_2_, f32[128,128]{1,0:T(8,128)S(1)} %collective-permute-done.21.refs_3_, ...), custom_call_target="tpu_custom_call" | custom-call | tf_op jit(solution)/shard_map/pallas_call | solution.py:105
  (55 shorter events, 9.5 us)
Async XLA Ops:
  3.2 10.7 %collective-permute-start = (f32[80,256]{1,0:T(8,128)S(1)}, f32[80,256]{1,0:T(8,128)S(1)}, u32[]{:S(2)}, u32[]{:S(2)}) collective-permute-start(f32[80,256]{1,0:T(8,128)S(1)} %get-tuple-element.53), channel_id=1, source_target_pairs={{0,3},{1,0},{2,1},{3,2},{4,7},{5,4},{6,5},{7,6},{8,11},{9,8},{10,9... | collective-permute-start | bytes 245768 | tf_op jit(solution)/shard_map/ppermute | solution.py:637
  8.3 7.9 %collective-permute-start.1 = (f32[80,256]{1,0:T(8,128)S(1)}, f32[80,256]{1,0:T(8,128)S(1)}, u32[]{:S(2)}, u32[]{:S(2)}) collective-permute-start(f32[80,256]{1,0:T(8,128)S(1)} %get-tuple-element.54), channel_id=1, source_target_pairs={{0,2},{1,3},{2,0},{3,1},{4,6},{5,7},{6,4},{7,5},{8,10},{9,11},{10,... | collective-permute-start | bytes 245768 | tf_op jit(solution)/shard_map/ppermute | solution.py:637
  8.3 7.9 %collective-permute-start.2 = (f32[80,256]{1,0:T(8,128)S(1)}, f32[80,256]{1,0:T(8,128)S(1)}, u32[]{:S(2)}, u32[]{:S(2)}) collective-permute-start(f32[80,256]{1,0:T(8,128)S(1)} %get-tuple-element.55), channel_id=1, source_target_pairs={{0,1},{1,2},{2,3},{3,0},{4,5},{5,6},{6,7},{7,4},{8,9},{9,10},{10,1... | collective-permute-start | bytes 245768 | tf_op jit(solution)/shard_map/ppermute | solution.py:637
  9.3 3.9 %copy-start.2 = (f32[3]{0:T(128)S(1)}, f32[3]{0:T(128)}, u32[]{:S(2)}) copy-start(f32[3]{0:T(128)} %param.10) | copy-start | bytes 40
  9.3 10.3 %collective-permute-start.3 = (f32[128,256]{1,0:T(8,128)S(1)}, f32[128,256]{1,0:T(8,128)S(1)}, u32[]{:S(2)}, u32[]{:S(2)}) collective-permute-start(f32[128,256]{1,0:T(8,128)S(1)} %get-tuple-element.60), channel_id=1, source_target_pairs={{0,3},{1,0},{2,1},{3,2},{4,7},{5,4},{6,5},{7,6},{8,11},{9,8},{10,9... | collective-permute-start | bytes 393224 | tf_op jit(solution)/shard_map/ppermute | solution.py:637
  12.1 15.0 %collective-permute-start.4 = (f32[128,256]{1,0:T(8,128)S(1)}, f32[128,256]{1,0:T(8,128)S(1)}, u32[]{:S(2)}, u32[]{:S(2)}) collective-permute-start(f32[128,256]{1,0:T(8,128)S(1)} %get-tuple-element.61), channel_id=1, source_target_pairs={{0,2},{1,3},{2,0},{3,1},{4,6},{5,7},{6,4},{7,5},{8,10},{9,11},{10,... | collective-permute-start | bytes 393224 | tf_op jit(solution)/shard_map/ppermute | solution.py:637
  14.0 13.1 %collective-permute-start.5 = (f32[128,256]{1,0:T(8,128)S(1)}, f32[128,256]{1,0:T(8,128)S(1)}, u32[]{:S(2)}, u32[]{:S(2)}) collective-permute-start(f32[128,256]{1,0:T(8,128)S(1)} %get-tuple-element.62), channel_id=1, source_target_pairs={{0,1},{1,2},{2,3},{3,0},{4,5},{5,6},{6,7},{7,4},{8,9},{9,10},{10,1... | collective-permute-start | bytes 393224 | tf_op jit(solution)/shard_map/ppermute | solution.py:637
  17.1 13.8 %collective-permute-start.11 = (f32[24,128]{1,0:T(8,128)S(1)}, f32[24,128]{1,0:T(8,128)S(1)}, u32[]{:S(2)}, u32[]{:S(2)}) collective-permute-start(f32[24,128]{1,0:T(8,128)S(1)} %get-tuple-element.111), channel_id=1, source_target_pairs={{0,24},{4,28},{8,0},{12,4},{16,8},{20,12},{24,16},{28,20},{1,25},{... | collective-permute-start | bytes 36872 | tf_op jit(solution)/shard_map/ppermute | solution.py:637
  19.6 18.0 %collective-permute-start.6 = (f32[288,128]{1,0:T(8,128)S(1)}, f32[288,128]{1,0:T(8,128)S(1)}, u32[]{:S(2)}, u32[]{:S(2)}) collective-permute-start(f32[288,128]{1,0:T(8,128)S(1)} %get-tuple-element.65), channel_id=1, source_target_pairs={{0,4},{4,8},{8,12},{12,16},{16,20},{20,24},{24,28},{28,0},{1,5},{5... | collective-permute-start | bytes 442376 | tf_op jit(solution)/shard_map/ppermute | solution.py:637
  19.6 18.0 %collective-permute-start.7 = (f32[288,128]{1,0:T(8,128)S(1)}, f32[288,128]{1,0:T(8,128)S(1)}, u32[]{:S(2)}, u32[]{:S(2)}) collective-permute-start(f32[288,128]{1,0:T(8,128)S(1)} %get-tuple-element.66), channel_id=1, source_target_pairs={{0,28},{4,0},{8,4},{12,8},{16,12},{20,16},{24,20},{28,24},{1,29},{... | collective-permute-start | bytes 442376 | tf_op jit(solution)/shard_map/ppermute | solution.py:637
  28.2 9.5 %collective-permute-start.8 = (f32[480,128]{1,0:T(8,128)S(1)}, f32[480,128]{1,0:T(8,128)S(1)}, u32[]{:S(2)}, u32[]{:S(2)}) collective-permute-start(f32[480,128]{1,0:T(8,128)S(1)} %get-tuple-element.67), channel_id=1, source_target_pairs={{0,4},{4,8},{8,12},{12,16},{16,20},{20,24},{24,28},{28,0},{1,5},{5... | collective-permute-start | bytes 737288 | tf_op jit(solution)/shard_map/ppermute | solution.py:637
  28.2 9.4 %collective-permute-start.9 = (f32[480,128]{1,0:T(8,128)S(1)}, f32[480,128]{1,0:T(8,128)S(1)}, u32[]{:S(2)}, u32[]{:S(2)}) collective-permute-start(f32[480,128]{1,0:T(8,128)S(1)} %get-tuple-element.68), channel_id=1, source_target_pairs={{0,28},{4,0},{8,4},{12,8},{16,12},{20,16},{24,20},{28,24},{1,29},{... | collective-permute-start | bytes 737288 | tf_op jit(solution)/shard_map/ppermute | solution.py:637
  30.9 6.7 %collective-permute-start.10 = (f32[24,128]{1,0:T(8,128)S(1)}, f32[24,128]{1,0:T(8,128)S(1)}, u32[]{:S(2)}, u32[]{:S(2)}) collective-permute-start(f32[24,128]{1,0:T(8,128)S(1)} %get-tuple-element.112), channel_id=1, source_target_pairs={{0,8},{4,12},{8,16},{12,20},{16,24},{20,28},{24,0},{28,4},{1,9},{5... | collective-permute-start | bytes 36872 | tf_op jit(solution)/shard_map/ppermute | solution.py:637
  42.7 7.3 %collective-permute-start.12 = (f32[256,128]{1,0:T(8,128)S(1)}, f32[256,128]{1,0:T(8,128)S(1)}, u32[]{:S(2)}, u32[]{:S(2)}) collective-permute-start(f32[256,128]{1,0:T(8,128)S(1)} %get-tuple-element.73), channel_id=1, source_target_pairs={{0,4},{4,8},{8,12},{12,16},{16,20},{20,24},{24,28},{28,0},{1,5},{5... | collective-permute-start | bytes 393224 | tf_op jit(solution)/shard_map/ppermute | solution.py:637
  42.7 7.3 %collective-permute-start.13 = (f32[256,128]{1,0:T(8,128)S(1)}, f32[256,128]{1,0:T(8,128)S(1)}, u32[]{:S(2)}, u32[]{:S(2)}) collective-permute-start(f32[256,128]{1,0:T(8,128)S(1)} %get-tuple-element.74), channel_id=1, source_target_pairs={{0,28},{4,0},{8,4},{12,8},{16,12},{20,16},{24,20},{28,24},{1,29},{... | collective-permute-start | bytes 393224 | tf_op jit(solution)/shard_map/ppermute | solution.py:637
  45.4 4.5 %collective-permute-start.14 = (f32[8,128]{1,0:T(8,128)S(1)}, f32[8,128]{1,0:T(8,128)S(1)}, u32[]{:S(2)}, u32[]{:S(2)}) collective-permute-start(f32[8,128]{1,0:T(8,128)S(1)} %get-tuple-element.75), channel_id=1, source_target_pairs={{0,8},{4,12},{8,16},{12,20},{16,24},{20,28},{24,0},{28,4},{1,9},{5... | collective-permute-start | bytes 12296 | tf_op jit(solution)/shard_map/ppermute | solution.py:637
  45.4 4.6 %collective-permute-start.15 = (f32[8,128]{1,0:T(8,128)S(1)}, f32[8,128]{1,0:T(8,128)S(1)}, u32[]{:S(2)}, u32[]{:S(2)}) collective-permute-start(f32[8,128]{1,0:T(8,128)S(1)} %get-tuple-element.76), channel_id=1, source_target_pairs={{0,24},{4,28},{8,0},{12,4},{16,8},{20,12},{24,16},{28,20},{1,25},{... | collective-permute-start | bytes 12296 | tf_op jit(solution)/shard_map/ppermute | solution.py:637
  54.6 8.3 %collective-permute-start.16 = (f32[256,128]{1,0:T(8,128)S(1)}, f32[256,128]{1,0:T(8,128)S(1)}, u32[]{:S(2)}, u32[]{:S(2)}) collective-permute-start(f32[256,128]{1,0:T(8,128)S(1)} %get-tuple-element.94), channel_id=1, source_target_pairs={{0,4},{4,8},{8,12},{12,16},{16,20},{20,24},{24,28},{28,0},{1,5},{5... | collective-permute-start | bytes 393224 | tf_op jit(solution)/shard_map/ppermute | solution.py:637
  54.6 8.3 %collective-permute-start.17 = (f32[256,128]{1,0:T(8,128)S(1)}, f32[256,128]{1,0:T(8,128)S(1)}, u32[]{:S(2)}, u32[]{:S(2)}) collective-permute-start(f32[256,128]{1,0:T(8,128)S(1)} %get-tuple-element.95), channel_id=1, source_target_pairs={{0,28},{4,0},{8,4},{12,8},{16,12},{20,16},{24,20},{28,24},{1,29},{... | collective-permute-start | bytes 393224 | tf_op jit(solution)/shard_map/ppermute | solution.py:637
  57.2 5.0 %collective-permute-start.18 = (f32[8,128]{1,0:T(8,128)S(1)}, f32[8,128]{1,0:T(8,128)S(1)}, u32[]{:S(2)}, u32[]{:S(2)}) collective-permute-start(f32[8,128]{1,0:T(8,128)S(1)} %get-tuple-element.96), channel_id=1, source_target_pairs={{0,8},{4,12},{8,16},{12,20},{16,24},{20,28},{24,0},{28,4},{1,9},{5... | collective-permute-start | bytes 12296 | tf_op jit(solution)/shard_map/ppermute | solution.py:637
  59.2 3.6 %collective-permute-start.19 = (f32[8,128]{1,0:T(8,128)S(1)}, f32[8,128]{1,0:T(8,128)S(1)}, u32[]{:S(2)}, u32[]{:S(2)}) collective-permute-start(f32[8,128]{1,0:T(8,128)S(1)} %get-tuple-element.97), channel_id=1, source_target_pairs={{0,24},{4,28},{8,0},{12,4},{16,8},{20,12},{24,16},{28,20},{1,25},{... | collective-permute-start | bytes 12296 | tf_op jit(solution)/shard_map/ppermute | solution.py:637
  67.1 4.8 %collective-permute-start.20 = (f32[128,128]{1,0:T(8,128)S(1)}, f32[128,128]{1,0:T(8,128)S(1)}, u32[]{:S(2)}, u32[]{:S(2)}) collective-permute-start(f32[128,128]{1,0:T(8,128)S(1)} %get-tuple-element.99), channel_id=1, source_target_pairs={{0,3},{1,0},{2,1},{3,2},{4,7},{5,4},{6,5},{7,6},{8,11},{9,8},{10,9... | collective-permute-start | bytes 196616 | tf_op jit(solution)/shard_map/ppermute | solution.py:637
  68.1 5.9 %collective-permute-start.21 = (f32[128,128]{1,0:T(8,128)S(1)}, f32[128,128]{1,0:T(8,128)S(1)}, u32[]{:S(2)}, u32[]{:S(2)}) collective-permute-start(f32[128,128]{1,0:T(8,128)S(1)} %get-tuple-element.100), channel_id=1, source_target_pairs={{0,2},{1,3},{2,0},{3,1},{4,6},{5,7},{6,4},{7,5},{8,10},{9,11},{10,... | collective-permute-start | bytes 196616 | tf_op jit(solution)/shard_map/ppermute | solution.py:637
  69.9 6.1 %collective-permute-start.22 = (f32[128,128]{1,0:T(8,128)S(1)}, f32[128,128]{1,0:T(8,128)S(1)}, u32[]{:S(2)}, u32[]{:S(2)}) collective-permute-start(f32[128,128]{1,0:T(8,128)S(1)} %get-tuple-element.101), channel_id=1, source_target_pairs={{0,1},{1,2},{2,3},{3,0},{4,5},{5,6},{6,7},{7,4},{8,9},{9,10},{10,1... | collective-permute-start | bytes 196616 | tf_op jit(solution)/shard_map/ppermute | solution.py:637
  (2 other events, 4.6 us)
where the time goes:
time: 77.4 us; the launch traced here: 77.3 us
  starting transfers between devices  34.5 us (45%)
  waiting for transfers between devices  20.4 us (26%)
  Pallas kernels  18.6 us (24%)
  local copies, waits for them, and re-layouts  1.78 us (2%)
  other arithmetic  1.24 us (2%)
    ppermute x23, starting transfers between devices, ring(): lax.ppermute(value, axis, [(i, (i - by) % peers) for i in range(peers)])  34.5 us
    ppermute x23, waiting for transfers between devices, ring(): lax.ppermute(value, axis, [(i, (i - by) % peers) for i in range(peers)])  20.4 us
    pallas_call x7, Pallas kernels, vmem_call(): pl.pallas_call(kernel, out_shape=[jax.ShapeDtypeStruct(o, F32) for o in o...  18.6 us
  transfers between devices with their start and end apart: 23, of which 10 were waited for; matrix products, arithmetic and copies ran while one was open for 2% of the time, Pallas kernels for 3%

commit v1 on v0

--- a/solution.py
+++ b/solution.py
@@ -20,10 +20,6 @@
 YH = 64
 
 
-def dot(a, b):
-    return jnp.dot(a, b, precision=lax.Precision.HIGHEST, preferred_element_type=F32)
-
-
 def blocks(ref, rows):
     return jnp.concatenate([ref[b, rows, :] for b in range(ref.shape[0])], axis=1)
 
@@ -31,6 +27,27 @@
 def put_blocks(ref, rows, value):
     for b in range(ref.shape[0]):
         ref[b, rows, :] = value[:, 128 * b : 128 * b + 128]
+
+
+def thirds(v):
+    high = v.astype(jnp.bfloat16)
+    rest = v - high.astype(F32)
+    mid = rest.astype(jnp.bfloat16)
+    return high, mid, (rest - mid.astype(F32)).astype(jnp.bfloat16)
+
+
+def spread(v, pick):
+    parts = [jnp.dot(p, pick, preferred_element_type=F32) for p in thirds(v)]
+    return parts[0] + (parts[1] + parts[2])
+
+
+def gathered(pick, v):
+    parts = [jnp.dot(pick, p, preferred_element_type=F32) for p in thirds(v)]
+    return parts[0] + (parts[1] + parts[2])
+
+
+def chosen(test, value=1.0):
+    return jnp.where(test, value, 0.0).astype(F32).astype(jnp.bfloat16)
 
 
 def iota(shape, dim):
@@ -83,6 +100,7 @@
         self.NZm, self.NZl = self.NZ // 2, self.NZ // 4
         self.WYm, self.NYm, self.NYl = self.WY // 2, self.NY // 2, self.NY // 4
         self.CH = max(1, min(4, 64 // self.NZ))
+        self.unrolled = self.NZ <= 16
         self.PF = self.nx + 2 * OUT
         self.PM = self.nxm + 2 * MH
         self.PL = self.nxl + 2 * LH
@@ -123,12 +141,8 @@
 
 def pack_kernel(g, idx, near, *outs):
     s = idx[0]
-    lane_pick = jnp.where(
-        iota((g.NY, g.NYl), 0) // 4 == iota((g.NY, g.NYl), 1), 1.0, 0.0
-    ).astype(F32)
-    row_pick = jnp.where(
-        iota((g.nxl, g.nx), 1) // 4 == iota((g.nxl, g.nx), 0), 1.0 / 64.0, 0.0
-    ).astype(F32)
+    lane_pick = chosen(iota((g.NY, g.NYl), 0) // 4 == iota((g.NY, g.NYl), 1))
+    row_pick = chosen(iota((g.nxl, g.nx), 1) // 4 == iota((g.nxl, g.nx), 0), 1.0 / 64.0)
     base = g.nz * g.nx
     first, second = outs[: g.ns], outs[g.ns :]
     turns = []
@@ -150,7 +164,7 @@
             repeat(g, g.nz, row)
         for zl in range(g.nz // 4):
             col = arr[4 * zl] + arr[4 * zl + 1] + arr[4 * zl + 2] + arr[4 * zl + 3]
-            low = dot(row_pick, dot(col, lane_pick))
+            low = gathered(row_pick, spread(col, lane_pick))
             at = base + a * g.lowrows + zl * g.nxl
             for k in range(g.ns):
                 first[k][at : at + g.nxl, : g.NYl] = low
@@ -163,8 +177,7 @@
     v = v.reshape(planes // 2, 2, nz // 2, lanes)
     v = (v[:, 0] + v[:, 1]).reshape(planes // 2 * (nz // 2), lanes)
     half = (lanes, lanes // 2)
-    pick = jnp.where(iota(half, 0) // 2 == iota(half, 1), scale / 8.0, 0.0).astype(F32)
-    return dot(v, pick)
+    return spread(v, chosen(iota(half, 0) // 2 == iota(half, 1), scale / 8.0))
 
 
 def assemble_kernel(g, count, idx, *refs):
@@ -248,42 +261,64 @@
     lax.fori_loop(1, jnp.maximum(idx[3], idx[4]), turn, 0)
 
 
-def fine_sweeps(g, idx, tab, gi, c, D, K, y, d):
+def small_sweep(tab, j, grids):
+    for level, nz, (gi, c, D, K, y, d, t) in grids:
+        rows = c.shape[0]
+        t[nz : nz + rows, :] = zy_sum(c[...] * y[...], nz)
+    for level, nz, (gi, c, D, K, y, d, t) in grids:
+        rows = c.shape[0]
+        box = t[0:rows, :] + t[nz : nz + rows, :] + t[2 * nz : 2 * nz + rows, :]
+        e = gi[...] - D[...] * y[...] + K[...] * box
+        nd = tab[level, j] * d[...] + tab[level, MAXDEG + j] * e
+        d[...] = nd
+        y[...] = y[...] + nd
+
+
+def all_sweeps(g, idx, tab, gi_at, fine, mid, low):
+    _, c, D, K, y, d, _ = fine
     nz = g.NZ
+    grids = ((1, g.NZm, mid), (2, g.NZl, low))
+    for level, _, (gi, _, _, _, ys, ds, _) in grids:
+        ys[...] = gi[...] * tab[level, 0]
+        ds[...] = ys[...]
 
     def rows(p):
         return slice((OUT + p) * nz, (OUT + p + 1) * nz)
 
-    for p in range(-XH, g.nx + XH):
-        r = rows(p)
-        y[r, :] = gi[r, :] * tab[0, 0]
-        d[r, :] = y[r, :]
-    for j in range(1, MAXDEG):
+    def fine_sweep(j):
+        alpha, beta = tab[0, j], tab[0, MAXDEG + j]
         reach = MAXDEG - j
+        first, last = -reach - 1, g.nx + reach
+        held, sums = {}, {}
+        for p in range(first, last + 1):
+            held[p] = gi_at(p) * tab[0, 0] if j == 1 else y[rows(p), :]
+            sums[p] = zy_sum(c[rows(p), :] * held[p], nz)
+            q = p - 1
+            if q <= first:
+                continue
+            r = rows(q)
+            box = sums[q - 1] + sums[q] + sums[p]
+            e = gi_at(q) - D[r, :] * held[q] + K[r, :] * box
+            nd = alpha * (held[q] if j == 1 else d[r, :]) + beta * e
+            if j < MAXDEG - 1:
+                d[r, :] = nd
+            y[r, :] = held[q] + nd
+
+    fine_sweep(1)
+    small_sweep(tab, 1, grids)
+    for j in range(2, MAXDEG):
 
         @pl.when(j < idx[2])
-        def _(j=j, reach=reach):
-            alpha, beta = tab[0, j], tab[0, MAXDEG + j]
-            first, last = -reach - 1, g.nx + reach
-            held, sums = {}, {}
-            for p in range(first, last + 1):
-                held[p] = y[rows(p), :]
-                sums[p] = zy_sum(c[rows(p), :] * held[p], nz)
-                q = p - 1
-                if q <= first:
-                    continue
-                r = rows(q)
-                box = sums[q - 1] + sums[q] + sums[p]
-                e = gi[r, :] - D[r, :] * held[q] + K[r, :] * box
-                nd = alpha * d[r, :] + beta * e
-                d[r, :] = nd
-                y[r, :] = held[q] + nd
+        def _(j=j):
+            fine_sweep(j)
+            small_sweep(tab, j, grids)
+
+        @pl.when((j >= idx[2]) & (j < jnp.maximum(idx[3], idx[4])))
+        def _(j=j):
+            small_sweep(tab, j, grids)
 
 
 def fine_smooth(g, idx, tab, gi, c, D, K, y, d, t):
-    if g.NZ <= 16:
-        fine_sweeps(g, idx, tab, gi, c, D, K, y, d)
-        return
     n = g.CH * g.NZ
     side, own = OUT // g.CH, g.nx // g.CH
     y[...] = gi[...] * tab[0, 0]
@@ -336,25 +371,21 @@
 
 def coarse_correction(g, s, ym, yl, zd):
     planes = g.nxm + 2
-    rows = planes * g.NZm
-    shape = (rows, g.PL * g.NZl)
+    shape = (g.WYm, g.WY)
+    mid_lanes = chosen(iota(shape, 0) == iota(shape, 1) // 2)
+    shape = (g.NYl, g.WY)
+    low_lanes = chosen(iota(shape, 0) == g.start(s) // 4 + iota(shape, 1) // 4)
+    first = (MH - 1) * g.NZm
+    mid = spread(ym[first : first + planes * g.NZm, :], mid_lanes)
+    low = spread(yl[...], low_lanes)
+    shape = (planes * g.NZm, g.PL * g.NZl)
     row, col = iota(shape, 0), iota(shape, 1)
     plane = row // g.NZm + (2 * LH - 1)
     want = (plane // 2) * g.NZl + (row % g.NZm) // 2
-    up_rows = jnp.where(col == want, 1.0, 0.0).astype(F32)
-    shape = (g.NYl, g.WYm)
-    off = g.start(s) // 4
-    up_lanes = jnp.where(
-        iota(shape, 0) == off + iota(shape, 1) // 2, 1.0, 0.0
-    ).astype(F32)
-    low = dot(dot(up_rows, yl[...]), up_lanes)
-    at = (MH - 1) * g.NZm
-    both = ym[at : at + rows, :] + low
-    shape = (g.WYm, g.WY)
-    wide = jnp.where(iota(shape, 0) == iota(shape, 1) // 2, 1.0, 0.0).astype(F32)
-    v = dot(both, wide)
-    put_blocks(zd, pl.ds(0, rows, stride=2), v)
-    put_blocks(zd, pl.ds(1, rows, stride=2), v)
+    v = mid + gathered(chosen(col == want), low)
+    n = planes * g.NZm
+    put_blocks(zd, pl.ds(0, n, stride=2), v)
+    put_blocks(zd, pl.ds(1, n, stride=2), v)
 
 
 def doubled(g, zd, plane, planes):
@@ -370,10 +401,13 @@
     return [(-1, 1)] + [(p, g.CH) for p in range(0, g.nx, g.CH)] + [(g.nx, 1)]
 
 
-def cycle(g, idx, tab, fine, mid, low, x_old, x, bi, diag, zd, keep, xb=None):
+def cycle(g, idx, tab, gi_at, fine, mid, low, x_old, x, bi, diag, zd, keep, xb=None):
     _, c, D, K, y, _, t = fine
-    fine_smooth(g, idx, tab, *fine)
-    coarse_smooth(g, idx, tab, mid, low)
+    if g.unrolled:
+        all_sweeps(g, idx, tab, gi_at, fine, mid, low)
+    else:
+        fine_smooth(g, idx, tab, *fine)
+        coarse_smooth(g, idx, tab, mid, low)
     coarse_correction(g, idx[0], mid[4], low[4], zd)
     for p, planes in pieces(g):
         n = planes * g.NZ
@@ -406,11 +440,11 @@
     row, col = iota(shape, 0), iota(shape, 1)
     same_x = col // (2 * g.NZm) == row // g.NZl
     same_z = (col % g.NZm) // 2 == row % g.NZl
-    rows = jnp.where(same_x & same_z, 0.5, 0.0).astype(F32)
+    rows = chosen(same_x & same_z, 0.5)
     shape = (g.WYm, g.NYl)
     off = g.start(s) // 4
-    lanes = jnp.where(iota(shape, 0) // 2 + off == iota(shape, 1), 1.0, 0.0).astype(F32)
-    rl[...] = dot(dot(rows, rm[...]), lanes)
+    lanes = chosen(iota(shape, 0) // 2 + off == iota(shape, 1))
+    rl[...] = spread(gathered(rows, rm[...]), lanes)
     at = 0
     for ref, n in ((gi, XH * g.NZ), (rm, MH * g.NZm), (rl, g.nxl * g.NZl)):
         total = ref.shape[0]
@@ -525,22 +559,27 @@
     fine = (gi, c, D, K, y, d, t)
     mid = (gm, cm, Dm, Km, ym, dm, tm)
     low = (gl, cl, Dl, Kl, yl, dl, tl)
-    cycle(g, idx, tab, fine, mid, low, None, x, bi, diag, zd, keep)
+
+    def gi_at(p):
+        return gi[(OUT + p) * g.NZ : (OUT + p + 1) * g.NZ, :]
+
+    cycle(g, idx, tab, gi_at, fine, mid, low, None, x, bi, diag, zd, keep)
     send_defect(g, s, gi_own, rm, rl, res, to_l, to_r, to_l2, to_r2)
 
 
 def gather_defect(g, gi_own, rm, rl, from_l, from_r, from_l2, from_r2, gi, gm, im, gl, il):
     lo, hi = OUT * g.NZ, (OUT + g.nx) * g.NZ
     n = XH * g.NZ
-    zeros = jnp.zeros((lo - n, g.WY), F32)
-    gi[0 : lo - n, :] = zeros
-    gi[hi + n :, :] = zeros
-    gi[lo:hi, :] = gi_own[...]
-    at = 0
-    for y in range(0, g.WY, 128):
-        gi[lo - n : lo, y : y + 128] = from_l[at : at + n, :]
-        gi[hi : hi + n, y : y + 128] = from_r[at : at + n, :]
-        at += n
+    at = 0 if not g.unrolled else g.WY // 128 * n
+    if not g.unrolled:
+        zeros = jnp.zeros((lo - n, g.WY), F32)
+        gi[0 : lo - n, :] = zeros
+        gi[hi + n :, :] = zeros
+        gi[lo:hi, :] = gi_own[...]
+        for y in range(0, g.WY, 128):
+            gi[lo - n : lo, y : y + 128] = from_l[at : at + n, :]
+            gi[hi : hi + n, y : y + 128] = from_r[at : at + n, :]
+            at += n
     n, own = MH * g.NZm, rm.shape[0]
     for y in range(0, g.WYm, 128):
         lanes = slice(y, y + 128)
@@ -575,6 +614,18 @@
     mid = (gm, cm, Dm, Km, ym, dm, tm)
     low = (gl, cl, Dl, Kl, yl, dl, tl)
     s = idx[0]
+
+    def gi_at(p):
+        if 0 <= p < g.nx:
+            return gi_own[p * g.NZ : (p + 1) * g.NZ, :]
+        part = received[0] if p < 0 else received[1]
+        at = (p + XH if p < 0 else p - g.nx) * g.NZ
+        step = XH * g.NZ
+        return jnp.concatenate(
+            [part[at + b * step : at + b * step + g.NZ, :] for b in range(g.WY // 128)],
+            axis=1,
+        )
+
     if len(scr) == 14:
         x, gi_new, rm_new, rl_new = outs[:4]
 
@@ -582,7 +633,7 @@
             gi_new[r, :] = scaled
             put_blocks(res, r, plain)
 
-        cycle(g, idx, tab, fine, mid, low, x_old, x, bi, diag, zd, keep)
+        cycle(g, idx, tab, gi_at, fine, mid, low, x_old, x, bi, diag, zd, keep)
         send_defect(g, s, gi_new, rm_new, rl_new, res, *outs[4:])
         return
     x, xb = scr[14:]
@@ -590,7 +641,7 @@
     def keep_plain(r, scaled, plain):
         put_blocks(res, r, plain)
 
-    cycle(g, idx, tab, fine, mid, low, x_old, x, bi, diag, zd, keep_plain, xb)
+    cycle(g, idx, tab, gi_at, fine, mid, low, x_old, x, bi, diag, zd, keep_plain, xb)
     shift = lax.rem(g.WY - (s * g.ny - g.start(s)), g.WY)
     for k in range(g.ns):
         partner = lax.rem(s - k + g.ns, g.ns)

time: 77.4 us -> 75.2 us (0.972)
  Pallas kernels: 18.6 us -> 16.4 us
    pallas_call x7, Pallas kernels: 18.6 us -> 16.4 us  [vmem_call(): pl.pallas_call(kernel, out_shape=[jax.ShapeDtypeStruct(o, F32) for o in o...]
  transfers between devices with their start and end apart: 23 -> 23, of which waited for: 10 -> 10; matrix products, arithmetic and copies ran while one was open for 2% -> 2% of each run, Pallas kernels for 3% -> 2%
where the time goes in v1:
time: 75.2 us; the launch traced here: 75 us
  starting transfers between devices  34.4 us (46%)
  waiting for transfers between devices  20.5 us (27%)
  Pallas kernels  16.4 us (22%)
  local copies, waits for them, and re-layouts  1.78 us (2%)
  other arithmetic  1.24 us (2%)
  between operations  0.76 us (1%)
    ppermute x23, starting transfers between devices, ring(): lax.ppermute(value, axis, [(i, (i - by) % peers) for i in range(peers)])  34.4 us
    ppermute x23, waiting for transfers between devices, ring(): lax.ppermute(value, axis, [(i, (i - by) % peers) for i in range(peers)])  20.5 us
    pallas_call x7, Pallas kernels, vmem_call(): pl.pallas_call(kernel, out_shape=[jax.ShapeDtypeStruct(o, F32) for o in o...  16.4 us
  transfers between devices with their start and end apart: 23, of which 10 were waited for; matrix products, arithmetic and copies ran while one was open for 2% of the time, Pallas kernels for 2%

profile of v1, /device:TPU:0, one launch (start us, length us, event | category | flops | bytes accessed | tf_op | source)
XLA Modules:
  0.0 75.0 jit_solution(1965868026786915092)
XLA Ops:
  1.8 1.2 %shard_map.77 = (f32[80,256]{1,0:T(8,128)S(1)}, f32[80,256]{1,0:T(8,128)S(1)}, f32[80,256]{1,0:T(8,128)S(1)}, f32[80,256]{1,0:T(8,128)S(1)}, f32[128,256]{1,0:T(...) custom-call(s32[2]{0:T(128)S(1)} %pad_add_fusion.refs_0_, ...), custom_call_target="tpu_custom_call" | custom-call | tf_op jit(solution)/shard_map/pallas_call | solution.py:123
  3.0 5.1 %collective-permute-start = (f32[80,256]{1,0:T(8,128)S(1)}, f32[80,256]{1,0:T(8,128)S(1)}, u32[]{:S(2)}, u32[]{:S(2)}) collective-permute-start(f32[80,256]{1,0:T(8,128)S(1)} %get-tuple-element.53), channel_id=1, source_target_pairs={{0,3},{1,0},{2,1},{3,2},{4,7},{5,4},{6,5},{7,6},{8,11},{9,8},{10,9... | collective-permute-start | bytes 245768 | tf_op jit(solution)/shard_map/ppermute | solution.py:688
  9.1 2.8 %collective-permute-start.3 = (f32[128,256]{1,0:T(8,128)S(1)}, f32[128,256]{1,0:T(8,128)S(1)}, u32[]{:S(2)}, u32[]{:S(2)}) collective-permute-start(f32[128,256]{1,0:T(8,128)S(1)} %get-tuple-element.60), channel_id=1, source_target_pairs={{0,3},{1,0},{2,1},{3,2},{4,7},{5,4},{6,5},{7,6},{8,11},{9,8},{10,9... | collective-permute-start | bytes 393224 | tf_op jit(solution)/shard_map/ppermute | solution.py:688
  11.9 1.1 %collective-permute-start.4 = (f32[128,256]{1,0:T(8,128)S(1)}, f32[128,256]{1,0:T(8,128)S(1)}, u32[]{:S(2)}, u32[]{:S(2)}) collective-permute-start(f32[128,256]{1,0:T(8,128)S(1)} %get-tuple-element.61), channel_id=1, source_target_pairs={{0,2},{1,3},{2,0},{3,1},{4,6},{5,7},{6,4},{7,5},{8,10},{9,11},{10,... | collective-permute-start | bytes 393224 | tf_op jit(solution)/shard_map/ppermute | solution.py:688
  13.8 2.2 %collective-permute-done.1.refs_3_ = f32[80,256]{1,0:T(8,128)S(1)} collective-permute-done((f32[80,256]{1,0:T(8,128)S(1)}, f32[80,256]{1,0:T(8,128)S(1)}, u32[]{:S(2)}, u32[]{:S(2)}) %collective-permute-start.1) | collective-permute-done | bytes 81952 | tf_op jit(solution)/shard_map/ppermute | solution.py:688
  16.9 2.5 %collective-permute-start.11 = (f32[24,128]{1,0:T(8,128)S(1)}, f32[24,128]{1,0:T(8,128)S(1)}, u32[]{:S(2)}, u32[]{:S(2)}) collective-permute-start(f32[24,128]{1,0:T(8,128)S(1)} %get-tuple-element.111), channel_id=1, source_target_pairs={{0,24},{4,28},{8,0},{12,4},{16,8},{20,12},{24,16},{28,20},{1,25},{... | collective-permute-start | bytes 36872 | tf_op jit(solution)/shard_map/ppermute | solution.py:688
  19.4 2.6 %collective-permute-start.7 = (f32[288,128]{1,0:T(8,128)S(1)}, f32[288,128]{1,0:T(8,128)S(1)}, u32[]{:S(2)}, u32[]{:S(2)}) collective-permute-start(f32[288,128]{1,0:T(8,128)S(1)} %get-tuple-element.66), channel_id=1, source_target_pairs={{0,28},{4,0},{8,4},{12,8},{16,12},{20,16},{24,20},{28,24},{1,29},{... | collective-permute-start | bytes 442376 | tf_op jit(solution)/shard_map/ppermute | solution.py:688
  22.0 4.9 %collective-permute-done.4.refs_3_ = f32[128,256]{1,0:T(8,128)S(1)} collective-permute-done((f32[128,256]{1,0:T(8,128)S(1)}, f32[128,256]{1,0:T(8,128)S(1)}, u32[]{:S(2)}, u32[]{:S(2)}) %collective-permute-start.4) | collective-permute-done | bytes 131104 | tf_op jit(solution)/shard_map/ppermute | solution.py:688
  28.0 2.6 %collective-permute-start.9 = (f32[480,128]{1,0:T(8,128)S(1)}, f32[480,128]{1,0:T(8,128)S(1)}, u32[]{:S(2)}, u32[]{:S(2)}) collective-permute-start(f32[480,128]{1,0:T(8,128)S(1)} %get-tuple-element.68), channel_id=1, source_target_pairs={{0,28},{4,0},{8,4},{12,8},{16,12},{20,16},{24,20},{28,24},{1,29},{... | collective-permute-start | bytes 737288 | tf_op jit(solution)/shard_map/ppermute | solution.py:688
  32.5 4.9 %collective-permute-done.10.refs_11_ = f32[24,128]{1,0:T(8,128)S(1)} collective-permute-done((f32[24,128]{1,0:T(8,128)S(1)}, f32[24,128]{1,0:T(8,128)S(1)}, u32[]{:S(2)}, u32[]{:S(2)}) %collective-permute-start.10) | collective-permute-done | bytes 12320 | tf_op jit(solution)/shard_map/ppermute | solution.py:688
  37.4 4.2 %shard_map.80 = (f32[512,256]{1,0:T(8,128)S(1)}, f32[512,256]{1,0:T(8,128)S(1)}, f32[512,256]{1,0:T(8,128)S(1)}, f32[256,256]{1,0:T(8,128)S(1)}, f32[256,256]{1,...) custom-call(s32[5]{0:T(128)S(1)} %pad_add_fusion.1.refs_0_, ...), custom_call_target="tpu_custom_call" | custom-call | tf_op jit(solution)/shard_map/pallas_call | solution.py:123
  41.6 2.7 %collective-permute-start.13 = (f32[256,128]{1,0:T(8,128)S(1)}, f32[256,128]{1,0:T(8,128)S(1)}, u32[]{:S(2)}, u32[]{:S(2)}) collective-permute-start(f32[256,128]{1,0:T(8,128)S(1)} %get-tuple-element.74), channel_id=1, source_target_pairs={{0,28},{4,0},{8,4},{12,8},{16,12},{20,16},{24,20},{28,24},{1,29},{... | collective-permute-start | bytes 393224 | tf_op jit(solution)/shard_map/ppermute | solution.py:688
  44.3 2.9 %collective-permute-start.15 = (f32[8,128]{1,0:T(8,128)S(1)}, f32[8,128]{1,0:T(8,128)S(1)}, u32[]{:S(2)}, u32[]{:S(2)}) collective-permute-start(f32[8,128]{1,0:T(8,128)S(1)} %get-tuple-element.76), channel_id=1, source_target_pairs={{0,24},{4,28},{8,0},{12,4},{16,8},{20,12},{24,16},{28,20},{1,25},{... | collective-permute-start | bytes 12296 | tf_op jit(solution)/shard_map/ppermute | solution.py:688
  47.2 1.6 %collective-permute-done.14.refs_8_ = f32[8,128]{1,0:T(8,128)S(1)} collective-permute-done((f32[8,128]{1,0:T(8,128)S(1)}, f32[8,128]{1,0:T(8,128)S(1)}, u32[]{:S(2)}, u32[]{:S(2)}) %collective-permute-start.14) | collective-permute-done | bytes 4128 | tf_op jit(solution)/shard_map/ppermute | solution.py:688
  48.9 4.0 %shard_map.81 = (f32[288,256]{1,0:T(8,128)S(1)}, f32[256,256]{1,0:T(8,128)S(1)}, f32[64,128]{1,0:T(8,128)S(1)}, f32[16,128]{1,0:T(8,128)S(1)}, f32[256,128]{1,0:...) custom-call(s32[5]{0:T(128)S(1)} %pad_add_fusion.1.refs_0_, ...), custom_call_target="tpu_custom_call" | custom-call | tf_op jit(solution)/shard_map/pallas_call | solution.py:123
  52.9 2.7 %collective-permute-start.17 = (f32[256,128]{1,0:T(8,128)S(1)}, f32[256,128]{1,0:T(8,128)S(1)}, u32[]{:S(2)}, u32[]{:S(2)}) collective-permute-start(f32[256,128]{1,0:T(8,128)S(1)} %get-tuple-element.95), channel_id=1, source_target_pairs={{0,28},{4,0},{8,4},{12,8},{16,12},{20,16},{24,20},{28,24},{1,29},{... | collective-permute-start | bytes 393224 | tf_op jit(solution)/shard_map/ppermute | solution.py:688
  55.5 2.0 %collective-permute-start.18 = (f32[8,128]{1,0:T(8,128)S(1)}, f32[8,128]{1,0:T(8,128)S(1)}, u32[]{:S(2)}, u32[]{:S(2)}) collective-permute-start(f32[8,128]{1,0:T(8,128)S(1)} %get-tuple-element.96), channel_id=1, source_target_pairs={{0,8},{4,12},{8,16},{12,20},{16,24},{20,28},{24,0},{28,4},{1,9},{5... | collective-permute-start | bytes 12296 | tf_op jit(solution)/shard_map/ppermute | solution.py:688
  58.5 2.1 %collective-permute-done.18.refs_8_ = f32[8,128]{1,0:T(8,128)S(1)} collective-permute-done((f32[8,128]{1,0:T(8,128)S(1)}, f32[8,128]{1,0:T(8,128)S(1)}, u32[]{:S(2)}, u32[]{:S(2)}) %collective-permute-start.18) | collective-permute-done | bytes 4128 | tf_op jit(solution)/shard_map/ppermute | solution.py:688
  61.1 3.7 %shard_map.82 = (f32[128,128]{1,0:T(8,128)S(1)}, f32[128,128]{1,0:T(8,128)S(1)}, f32[128,128]{1,0:T(8,128)S(1)}, f32[128,128]{1,0:T(8,128)S(1)}) custom-call(s32[5]{0:T(128)S(1)} %pad_add_fusion.1.refs_0_, f32[3,12]{1,0:T(4,128)S(1)} %stack.71.refs_1_, f32[256,256]{1,0:T(8,128)S(1)} %get-tuple-element.90.refs_2_, f32[64,128]{1,0:T(8,128)S(1)} %get-tuple-element.91.refs_3_, ...), custom_call_target="tpu_custom_call" | custom-call | tf_op jit(solution)/shard_map/pallas_call | solution.py:123
  65.9 1.7 %collective-permute-start.21 = (f32[128,128]{1,0:T(8,128)S(1)}, f32[128,128]{1,0:T(8,128)S(1)}, u32[]{:S(2)}, u32[]{:S(2)}) collective-permute-start(f32[128,128]{1,0:T(8,128)S(1)} %get-tuple-element.100), channel_id=1, source_target_pairs={{0,2},{1,3},{2,0},{3,1},{4,6},{5,7},{6,4},{7,5},{8,10},{9,11},{10,... | collective-permute-start | bytes 196616 | tf_op jit(solution)/shard_map/ppermute | solution.py:688
  67.6 1.9 %collective-permute-start.22 = (f32[128,128]{1,0:T(8,128)S(1)}, f32[128,128]{1,0:T(8,128)S(1)}, u32[]{:S(2)}, u32[]{:S(2)}) collective-permute-start(f32[128,128]{1,0:T(8,128)S(1)} %get-tuple-element.101), channel_id=1, source_target_pairs={{0,1},{1,2},{2,3},{3,0},{4,5},{5,6},{6,7},{7,4},{8,9},{9,10},{10,1... | collective-permute-start | bytes 196616 | tf_op jit(solution)/shard_map/ppermute | solution.py:688
  69.7 2.1 %collective-permute-done.21.refs_3_ = f32[128,128]{1,0:T(8,128)S(1)} collective-permute-done((f32[128,128]{1,0:T(8,128)S(1)}, f32[128,128]{1,0:T(8,128)S(1)}, u32[]{:S(2)}, u32[]{:S(2)}) %collective-permute-start.21) | collective-permute-done | bytes 65568 | tf_op jit(solution)/shard_map/ppermute | solution.py:688
  71.8 1.9 %collective-permute-done.22.refs_4_ = f32[128,128]{1,0:T(8,128)S(1)} collective-permute-done((f32[128,128]{1,0:T(8,128)S(1)}, f32[128,128]{1,0:T(8,128)S(1)}, u32[]{:S(2)}, u32[]{:S(2)}) %collective-permute-start.22) | collective-permute-done | bytes 65568 | tf_op jit(solution)/shard_map/ppermute | solution.py:688
  73.7 1.3 %shard_map.83 = (f32[4,16,512]{2,1,0:T(8,128)}, f32[4,16,512]{2,1,0:T(8,128)}) custom-call(s32[2]{0:T(128)S(1)} %pad_add_fusion.refs_0_, f32[128,128]{1,0:T(8,128)S(1)} %get-tuple-element.98.refs_1_, f32[128,128]{1,0:T(8,128)S(1)} %collective-permute-done.20.refs_2_, f32[128,128]{1,0:T(8,128)S(1)} %collective-permute-done.21.refs_3_, ...), custom_call_target="tpu_custom_call" | custom-call | tf_op jit(solution)/shard_map/pallas_call | solution.py:123
  (55 shorter events, 9.4 us)
Async XLA Ops:
  3.0 10.7 %collective-permute-start = (f32[80,256]{1,0:T(8,128)S(1)}, f32[80,256]{1,0:T(8,128)S(1)}, u32[]{:S(2)}, u32[]{:S(2)}) collective-permute-start(f32[80,256]{1,0:T(8,128)S(1)} %get-tuple-element.53), channel_id=1, source_target_pairs={{0,3},{1,0},{2,1},{3,2},{4,7},{5,4},{6,5},{7,6},{8,11},{9,8},{10,9... | collective-permute-start | bytes 245768 | tf_op jit(solution)/shard_map/ppermute | solution.py:688
  8.1 7.9 %collective-permute-start.1 = (f32[80,256]{1,0:T(8,128)S(1)}, f32[80,256]{1,0:T(8,128)S(1)}, u32[]{:S(2)}, u32[]{:S(2)}) collective-permute-start(f32[80,256]{1,0:T(8,128)S(1)} %get-tuple-element.54), channel_id=1, source_target_pairs={{0,2},{1,3},{2,0},{3,1},{4,6},{5,7},{6,4},{7,5},{8,10},{9,11},{10,... | collective-permute-start | bytes 245768 | tf_op jit(solution)/shard_map/ppermute | solution.py:688
  8.1 7.9 %collective-permute-start.2 = (f32[80,256]{1,0:T(8,128)S(1)}, f32[80,256]{1,0:T(8,128)S(1)}, u32[]{:S(2)}, u32[]{:S(2)}) collective-permute-start(f32[80,256]{1,0:T(8,128)S(1)} %get-tuple-element.55), channel_id=1, source_target_pairs={{0,1},{1,2},{2,3},{3,0},{4,5},{5,6},{6,7},{7,4},{8,9},{9,10},{10,1... | collective-permute-start | bytes 245768 | tf_op jit(solution)/shard_map/ppermute | solution.py:688
  9.1 3.9 %copy-start.2 = (f32[3]{0:T(128)S(1)}, f32[3]{0:T(128)}, u32[]{:S(2)}) copy-start(f32[3]{0:T(128)} %param.10) | copy-start | bytes 40
  9.1 10.2 %collective-permute-start.3 = (f32[128,256]{1,0:T(8,128)S(1)}, f32[128,256]{1,0:T(8,128)S(1)}, u32[]{:S(2)}, u32[]{:S(2)}) collective-permute-start(f32[128,256]{1,0:T(8,128)S(1)} %get-tuple-element.60), channel_id=1, source_target_pairs={{0,3},{1,0},{2,1},{3,2},{4,7},{5,4},{6,5},{7,6},{8,11},{9,8},{10,9... | collective-permute-start | bytes 393224 | tf_op jit(solution)/shard_map/ppermute | solution.py:688
  11.9 15.0 %collective-permute-start.4 = (f32[128,256]{1,0:T(8,128)S(1)}, f32[128,256]{1,0:T(8,128)S(1)}, u32[]{:S(2)}, u32[]{:S(2)}) collective-permute-start(f32[128,256]{1,0:T(8,128)S(1)} %get-tuple-element.61), channel_id=1, source_target_pairs={{0,2},{1,3},{2,0},{3,1},{4,6},{5,7},{6,4},{7,5},{8,10},{9,11},{10,... | collective-permute-start | bytes 393224 | tf_op jit(solution)/shard_map/ppermute | solution.py:688
  13.8 13.1 %collective-permute-start.5 = (f32[128,256]{1,0:T(8,128)S(1)}, f32[128,256]{1,0:T(8,128)S(1)}, u32[]{:S(2)}, u32[]{:S(2)}) collective-permute-start(f32[128,256]{1,0:T(8,128)S(1)} %get-tuple-element.62), channel_id=1, source_target_pairs={{0,1},{1,2},{2,3},{3,0},{4,5},{5,6},{6,7},{7,4},{8,9},{9,10},{10,1... | collective-permute-start | bytes 393224 | tf_op jit(solution)/shard_map/ppermute | solution.py:688
  16.9 13.8 %collective-permute-start.11 = (f32[24,128]{1,0:T(8,128)S(1)}, f32[24,128]{1,0:T(8,128)S(1)}, u32[]{:S(2)}, u32[]{:S(2)}) collective-permute-start(f32[24,128]{1,0:T(8,128)S(1)} %get-tuple-element.111), channel_id=1, source_target_pairs={{0,24},{4,28},{8,0},{12,4},{16,8},{20,12},{24,16},{28,20},{1,25},{... | collective-permute-start | bytes 36872 | tf_op jit(solution)/shard_map/ppermute | solution.py:688
  19.4 18.0 %collective-permute-start.6 = (f32[288,128]{1,0:T(8,128)S(1)}, f32[288,128]{1,0:T(8,128)S(1)}, u32[]{:S(2)}, u32[]{:S(2)}) collective-permute-start(f32[288,128]{1,0:T(8,128)S(1)} %get-tuple-element.65), channel_id=1, source_target_pairs={{0,4},{4,8},{8,12},{12,16},{16,20},{20,24},{24,28},{28,0},{1,5},{5... | collective-permute-start | bytes 442376 | tf_op jit(solution)/shard_map/ppermute | solution.py:688
  19.4 18.0 %collective-permute-start.7 = (f32[288,128]{1,0:T(8,128)S(1)}, f32[288,128]{1,0:T(8,128)S(1)}, u32[]{:S(2)}, u32[]{:S(2)}) collective-permute-start(f32[288,128]{1,0:T(8,128)S(1)} %get-tuple-element.66), channel_id=1, source_target_pairs={{0,28},{4,0},{8,4},{12,8},{16,12},{20,16},{24,20},{28,24},{1,29},{... | collective-permute-start | bytes 442376 | tf_op jit(solution)/shard_map/ppermute | solution.py:688
  27.9 9.5 %collective-permute-start.8 = (f32[480,128]{1,0:T(8,128)S(1)}, f32[480,128]{1,0:T(8,128)S(1)}, u32[]{:S(2)}, u32[]{:S(2)}) collective-permute-start(f32[480,128]{1,0:T(8,128)S(1)} %get-tuple-element.67), channel_id=1, source_target_pairs={{0,4},{4,8},{8,12},{12,16},{16,20},{20,24},{24,28},{28,0},{1,5},{5... | collective-permute-start | bytes 737288 | tf_op jit(solution)/shard_map/ppermute | solution.py:688
  28.0 9.4 %collective-permute-start.9 = (f32[480,128]{1,0:T(8,128)S(1)}, f32[480,128]{1,0:T(8,128)S(1)}, u32[]{:S(2)}, u32[]{:S(2)}) collective-permute-start(f32[480,128]{1,0:T(8,128)S(1)} %get-tuple-element.68), channel_id=1, source_target_pairs={{0,28},{4,0},{8,4},{12,8},{16,12},{20,16},{24,20},{28,24},{1,29},{... | collective-permute-start | bytes 737288 | tf_op jit(solution)/shard_map/ppermute | solution.py:688
  30.6 6.7 %collective-permute-start.10 = (f32[24,128]{1,0:T(8,128)S(1)}, f32[24,128]{1,0:T(8,128)S(1)}, u32[]{:S(2)}, u32[]{:S(2)}) collective-permute-start(f32[24,128]{1,0:T(8,128)S(1)} %get-tuple-element.112), channel_id=1, source_target_pairs={{0,8},{4,12},{8,16},{12,20},{16,24},{20,28},{24,0},{28,4},{1,9},{5... | collective-permute-start | bytes 36872 | tf_op jit(solution)/shard_map/ppermute | solution.py:688
  41.6 7.3 %collective-permute-start.12 = (f32[256,128]{1,0:T(8,128)S(1)}, f32[256,128]{1,0:T(8,128)S(1)}, u32[]{:S(2)}, u32[]{:S(2)}) collective-permute-start(f32[256,128]{1,0:T(8,128)S(1)} %get-tuple-element.73), channel_id=1, source_target_pairs={{0,4},{4,8},{8,12},{12,16},{16,20},{20,24},{24,28},{28,0},{1,5},{5... | collective-permute-start | bytes 393224 | tf_op jit(solution)/shard_map/ppermute | solution.py:688
  41.6 7.3 %collective-permute-start.13 = (f32[256,128]{1,0:T(8,128)S(1)}, f32[256,128]{1,0:T(8,128)S(1)}, u32[]{:S(2)}, u32[]{:S(2)}) collective-permute-start(f32[256,128]{1,0:T(8,128)S(1)} %get-tuple-element.74), channel_id=1, source_target_pairs={{0,28},{4,0},{8,4},{12,8},{16,12},{20,16},{24,20},{28,24},{1,29},{... | collective-permute-start | bytes 393224 | tf_op jit(solution)/shard_map/ppermute | solution.py:688
  44.3 4.5 %collective-permute-start.14 = (f32[8,128]{1,0:T(8,128)S(1)}, f32[8,128]{1,0:T(8,128)S(1)}, u32[]{:S(2)}, u32[]{:S(2)}) collective-permute-start(f32[8,128]{1,0:T(8,128)S(1)} %get-tuple-element.75), channel_id=1, source_target_pairs={{0,8},{4,12},{8,16},{12,20},{16,24},{20,28},{24,0},{28,4},{1,9},{5... | collective-permute-start | bytes 12296 | tf_op jit(solution)/shard_map/ppermute | solution.py:688
  44.3 4.6 %collective-permute-start.15 = (f32[8,128]{1,0:T(8,128)S(1)}, f32[8,128]{1,0:T(8,128)S(1)}, u32[]{:S(2)}, u32[]{:S(2)}) collective-permute-start(f32[8,128]{1,0:T(8,128)S(1)} %get-tuple-element.76), channel_id=1, source_target_pairs={{0,24},{4,28},{8,0},{12,4},{16,8},{20,12},{24,16},{28,20},{1,25},{... | collective-permute-start | bytes 12296 | tf_op jit(solution)/shard_map/ppermute | solution.py:688
  52.9 8.3 %collective-permute-start.16 = (f32[256,128]{1,0:T(8,128)S(1)}, f32[256,128]{1,0:T(8,128)S(1)}, u32[]{:S(2)}, u32[]{:S(2)}) collective-permute-start(f32[256,128]{1,0:T(8,128)S(1)} %get-tuple-element.94), channel_id=1, source_target_pairs={{0,4},{4,8},{8,12},{12,16},{16,20},{20,24},{24,28},{28,0},{1,5},{5... | collective-permute-start | bytes 393224 | tf_op jit(solution)/shard_map/ppermute | solution.py:688
  52.9 8.3 %collective-permute-start.17 = (f32[256,128]{1,0:T(8,128)S(1)}, f32[256,128]{1,0:T(8,128)S(1)}, u32[]{:S(2)}, u32[]{:S(2)}) collective-permute-start(f32[256,128]{1,0:T(8,128)S(1)} %get-tuple-element.95), channel_id=1, source_target_pairs={{0,28},{4,0},{8,4},{12,8},{16,12},{20,16},{24,20},{28,24},{1,29},{... | collective-permute-start | bytes 393224 | tf_op jit(solution)/shard_map/ppermute | solution.py:688
  55.5 5.0 %collective-permute-start.18 = (f32[8,128]{1,0:T(8,128)S(1)}, f32[8,128]{1,0:T(8,128)S(1)}, u32[]{:S(2)}, u32[]{:S(2)}) collective-permute-start(f32[8,128]{1,0:T(8,128)S(1)} %get-tuple-element.96), channel_id=1, source_target_pairs={{0,8},{4,12},{8,16},{12,20},{16,24},{20,28},{24,0},{28,4},{1,9},{5... | collective-permute-start | bytes 12296 | tf_op jit(solution)/shard_map/ppermute | solution.py:688
  57.5 3.6 %collective-permute-start.19 = (f32[8,128]{1,0:T(8,128)S(1)}, f32[8,128]{1,0:T(8,128)S(1)}, u32[]{:S(2)}, u32[]{:S(2)}) collective-permute-start(f32[8,128]{1,0:T(8,128)S(1)} %get-tuple-element.97), channel_id=1, source_target_pairs={{0,24},{4,28},{8,0},{12,4},{16,8},{20,12},{24,16},{28,20},{1,25},{... | collective-permute-start | bytes 12296 | tf_op jit(solution)/shard_map/ppermute | solution.py:688
  64.9 4.8 %collective-permute-start.20 = (f32[128,128]{1,0:T(8,128)S(1)}, f32[128,128]{1,0:T(8,128)S(1)}, u32[]{:S(2)}, u32[]{:S(2)}) collective-permute-start(f32[128,128]{1,0:T(8,128)S(1)} %get-tuple-element.99), channel_id=1, source_target_pairs={{0,3},{1,0},{2,1},{3,2},{4,7},{5,4},{6,5},{7,6},{8,11},{9,8},{10,9... | collective-permute-start | bytes 196616 | tf_op jit(solution)/shard_map/ppermute | solution.py:688
  65.9 5.9 %collective-permute-start.21 = (f32[128,128]{1,0:T(8,128)S(1)}, f32[128,128]{1,0:T(8,128)S(1)}, u32[]{:S(2)}, u32[]{:S(2)}) collective-permute-start(f32[128,128]{1,0:T(8,128)S(1)} %get-tuple-element.100), channel_id=1, source_target_pairs={{0,2},{1,3},{2,0},{3,1},{4,6},{5,7},{6,4},{7,5},{8,10},{9,11},{10,... | collective-permute-start | bytes 196616 | tf_op jit(solution)/shard_map/ppermute | solution.py:688
  67.6 6.1 %collective-permute-start.22 = (f32[128,128]{1,0:T(8,128)S(1)}, f32[128,128]{1,0:T(8,128)S(1)}, u32[]{:S(2)}, u32[]{:S(2)}) collective-permute-start(f32[128,128]{1,0:T(8,128)S(1)} %get-tuple-element.101), channel_id=1, source_target_pairs={{0,1},{1,2},{2,3},{3,0},{4,5},{5,6},{6,7},{7,4},{8,9},{9,10},{10,1... | collective-permute-start | bytes 196616 | tf_op jit(solution)/shard_map/ppermute | solution.py:688
  (2 other events, 4.6 us)

commit v2 on v1

--- a/solution.py
+++ b/solution.py
@@ -170,13 +170,16 @@
                 first[k][at : at + g.nxl, : g.NYl] = low
 
 
-def fine_to_mid(src, row, planes, nz, scale):
+def pair_sums(src, planes, nz):
     n = planes * nz // 2
     lanes = src.shape[0] * 128
-    v = blocks(src, pl.ds(row, n, stride=2)) + blocks(src, pl.ds(row + 1, n, stride=2))
+    v = blocks(src, pl.ds(0, n, stride=2)) + blocks(src, pl.ds(1, n, stride=2))
     v = v.reshape(planes // 2, 2, nz // 2, lanes)
-    v = (v[:, 0] + v[:, 1]).reshape(planes // 2 * (nz // 2), lanes)
-    half = (lanes, lanes // 2)
+    return (v[:, 0] + v[:, 1]).reshape(planes // 2 * (nz // 2), lanes)
+
+
+def to_mid(v, scale):
+    half = (v.shape[1], v.shape[1] // 2)
     return spread(v, chosen(iota(half, 0) // 2 == iota(half, 1), scale / 8.0))
 
 
@@ -209,7 +212,7 @@
     at, n = 0, XH * g.NZ
     for a in range(count):
         f_out[a] = blocks(fs.at[a], slice(0, nxz))
-        m_out[a] = fine_to_mid(fs.at[a], 0, g.nx, g.NZ, 1.0)
+        m_out[a] = to_mid(pair_sums(fs.at[a], g.nx, g.NZ), 1.0)
         for b in range(g.WY // 128):
             to_left[at : at + n, :] = fs[a, b, 0:n, :]
             to_right[at : at + n, :] = fs[a, b, nxz - n :, :]
@@ -274,7 +277,7 @@
         y[...] = y[...] + nd
 
 
-def all_sweeps(g, idx, tab, gi_at, fine, mid, low):
+def all_sweeps(g, idx, tab, gi_at, fine, mid, low, zd):
     _, c, D, K, y, d, _ = fine
     nz = g.NZ
     grids = ((1, g.NZm, mid), (2, g.NZl, low))
@@ -304,18 +307,29 @@
                 d[r, :] = nd
             y[r, :] = held[q] + nd
 
+    ahead = {j: () for j in range(1, MAXDEG)}
+    ahead[1], ahead[2], ahead[3] = (1, 2), (3, 4), (5,)
+
+    def beside(j):
+        for k in ahead[j]:
+            small_sweep(tab, k, grids)
+        if j == 4:
+            coarse_correction(g, idx[0], mid[4], low[4], zd)
+
     fine_sweep(1)
-    small_sweep(tab, 1, grids)
+    beside(1)
     for j in range(2, MAXDEG):
 
         @pl.when(j < idx[2])
         def _(j=j):
             fine_sweep(j)
-            small_sweep(tab, j, grids)
-
-        @pl.when((j >= idx[2]) & (j < jnp.maximum(idx[3], idx[4])))
-        def _(j=j):
-            small_sweep(tab, j, grids)
+            beside(j)
+
+        if j < 5:
+
+            @pl.when(j >= idx[2])
+            def _(j=j):
+                beside(j)
 
 
 def fine_smooth(g, idx, tab, gi, c, D, K, y, d, t):
@@ -404,11 +418,11 @@
 def cycle(g, idx, tab, gi_at, fine, mid, low, x_old, x, bi, diag, zd, keep, xb=None):
     _, c, D, K, y, _, t = fine
     if g.unrolled:
-        all_sweeps(g, idx, tab, gi_at, fine, mid, low)
+        all_sweeps(g, idx, tab, gi_at, fine, mid, low, zd)
     else:
         fine_smooth(g, idx, tab, *fine)
         coarse_smooth(g, idx, tab, mid, low)
-    coarse_correction(g, idx[0], mid[4], low[4], zd)
+        coarse_correction(g, idx[0], mid[4], low[4], zd)
     for p, planes in pieces(g):
         n = planes * g.NZ
         rr = slice((OUT + p) * g.NZ, (OUT + p) * g.NZ + n)
@@ -435,16 +449,16 @@
 
 
 def send_defect(g, s, gi, rm, rl, res, to_l, to_r, to_l2, to_r2):
-    rm[...] = fine_to_mid(res, 0, g.nx, g.NZ, 4.0)
+    sums = pair_sums(res, g.nx, g.NZ)
+    rm[...] = to_mid(sums, 4.0)
     shape = (g.nxl * g.NZl, g.nxm * g.NZm)
     row, col = iota(shape, 0), iota(shape, 1)
     same_x = col // (2 * g.NZm) == row // g.NZl
     same_z = (col % g.NZm) // 2 == row % g.NZl
-    rows = chosen(same_x & same_z, 0.5)
-    shape = (g.WYm, g.NYl)
-    off = g.start(s) // 4
-    lanes = chosen(iota(shape, 0) // 2 + off == iota(shape, 1))
-    rl[...] = spread(gathered(rows, rm[...]), lanes)
+    rows = chosen(same_x & same_z, 0.25)
+    shape = (g.WY, g.NYl)
+    lanes = chosen(iota(shape, 0) // 4 + g.start(s) // 4 == iota(shape, 1))
+    rl[...] = spread(gathered(rows, sums), lanes)
     at = 0
     for ref, n in ((gi, XH * g.NZ), (rm, MH * g.NZm), (rl, g.nxl * g.NZl)):
         total = ref.shape[0]
@@ -795,7 +809,9 @@
             shapes, scratch + more, 2,
             (idx, tab, gi, rm, rl, x, *received, *coefs),
         )
-    packs = [ring(v, "slab", k) for k, v in enumerate(outs)]
+    packs = []
+    for k, v in enumerate(outs):
+        packs.append(ring(v, "slab", k))
     return tuple(call(unpack_kernel, [shape, shape], [], 1, place, *packs))
 
 

time: 75.2 us -> 74.5 us (level)
  Pallas kernels: 16.4 us -> 15.6 us
where the time goes in v2:
time: 74.5 us; the launch traced here: 74.4 us
  starting transfers between devices  34.5 us (46%)
  waiting for transfers between devices  20.5 us (28%)
  Pallas kernels  15.6 us (21%)
  local copies, waits for them, and re-layouts  1.78 us (2%)
  other arithmetic  1.24 us (2%)
  between operations  0.78 us (1%)
    ppermute x23, starting transfers between devices, ring(): lax.ppermute(value, axis, [(i, (i - by) % peers) for i in range(peers)])  34.5 us
    ppermute x23, waiting for transfers between devices, ring(): lax.ppermute(value, axis, [(i, (i - by) % peers) for i in range(peers)])  20.5 us
    pallas_call x7, Pallas kernels, vmem_call(): pl.pallas_call(kernel, out_shape=[jax.ShapeDtypeStruct(o, F32) for o in o...  15.6 us
  transfers between devices with their start and end apart: 23, of which 10 were waited for; matrix products, arithmetic and copies ran while one was open for 2% of the time, Pallas kernels for 2%

profile of v2, /device:TPU:0, one launch (start us, length us, event | category | flops | bytes accessed | tf_op | source)
XLA Modules:
  0.0 74.4 jit_solution(10410271757974613582)
XLA Ops:
  1.8 1.2 %shard_map.77 = (f32[80,256]{1,0:T(8,128)S(1)}, f32[80,256]{1,0:T(8,128)S(1)}, f32[80,256]{1,0:T(8,128)S(1)}, f32[80,256]{1,0:T(8,128)S(1)}, f32[128,256]{1,0:T(...) custom-call(s32[2]{0:T(128)S(1)} %pad_add_fusion.refs_0_, ...), custom_call_target="tpu_custom_call" | custom-call | tf_op jit(solution)/shard_map/pallas_call | solution.py:123
  3.0 5.1 %collective-permute-start = (f32[80,256]{1,0:T(8,128)S(1)}, f32[80,256]{1,0:T(8,128)S(1)}, u32[]{:S(2)}, u32[]{:S(2)}) collective-permute-start(f32[80,256]{1,0:T(8,128)S(1)} %get-tuple-element.53), channel_id=1, source_target_pairs={{0,3},{1,0},{2,1},{3,2},{4,7},{5,4},{6,5},{7,6},{8,11},{9,8},{10,9... | collective-permute-start | bytes 245768 | tf_op jit(solution)/shard_map/ppermute | solution.py:702
  9.1 2.8 %collective-permute-start.3 = (f32[128,256]{1,0:T(8,128)S(1)}, f32[128,256]{1,0:T(8,128)S(1)}, u32[]{:S(2)}, u32[]{:S(2)}) collective-permute-start(f32[128,256]{1,0:T(8,128)S(1)} %get-tuple-element.60), channel_id=1, source_target_pairs={{0,3},{1,0},{2,1},{3,2},{4,7},{5,4},{6,5},{7,6},{8,11},{9,8},{10,9... | collective-permute-start | bytes 393224 | tf_op jit(solution)/shard_map/ppermute | solution.py:702
  11.9 1.1 %collective-permute-start.4 = (f32[128,256]{1,0:T(8,128)S(1)}, f32[128,256]{1,0:T(8,128)S(1)}, u32[]{:S(2)}, u32[]{:S(2)}) collective-permute-start(f32[128,256]{1,0:T(8,128)S(1)} %get-tuple-element.61), channel_id=1, source_target_pairs={{0,2},{1,3},{2,0},{3,1},{4,6},{5,7},{6,4},{7,5},{8,10},{9,11},{10,... | collective-permute-start | bytes 393224 | tf_op jit(solution)/shard_map/ppermute | solution.py:702
  13.8 2.2 %collective-permute-done.1.refs_3_ = f32[80,256]{1,0:T(8,128)S(1)} collective-permute-done((f32[80,256]{1,0:T(8,128)S(1)}, f32[80,256]{1,0:T(8,128)S(1)}, u32[]{:S(2)}, u32[]{:S(2)}) %collective-permute-start.1) | collective-permute-done | bytes 81952 | tf_op jit(solution)/shard_map/ppermute | solution.py:702
  16.9 2.5 %collective-permute-start.11 = (f32[24,128]{1,0:T(8,128)S(1)}, f32[24,128]{1,0:T(8,128)S(1)}, u32[]{:S(2)}, u32[]{:S(2)}) collective-permute-start(f32[24,128]{1,0:T(8,128)S(1)} %get-tuple-element.111), channel_id=1, source_target_pairs={{0,24},{4,28},{8,0},{12,4},{16,8},{20,12},{24,16},{28,20},{1,25},{... | collective-permute-start | bytes 36872 | tf_op jit(solution)/shard_map/ppermute | solution.py:702
  19.4 2.6 %collective-permute-start.7 = (f32[288,128]{1,0:T(8,128)S(1)}, f32[288,128]{1,0:T(8,128)S(1)}, u32[]{:S(2)}, u32[]{:S(2)}) collective-permute-start(f32[288,128]{1,0:T(8,128)S(1)} %get-tuple-element.66), channel_id=1, source_target_pairs={{0,28},{4,0},{8,4},{12,8},{16,12},{20,16},{24,20},{28,24},{1,29},{... | collective-permute-start | bytes 442376 | tf_op jit(solution)/shard_map/ppermute | solution.py:702
  22.0 4.9 %collective-permute-done.4.refs_3_ = f32[128,256]{1,0:T(8,128)S(1)} collective-permute-done((f32[128,256]{1,0:T(8,128)S(1)}, f32[128,256]{1,0:T(8,128)S(1)}, u32[]{:S(2)}, u32[]{:S(2)}) %collective-permute-start.4) | collective-permute-done | bytes 131104 | tf_op jit(solution)/shard_map/ppermute | solution.py:702
  28.0 2.6 %collective-permute-start.9 = (f32[480,128]{1,0:T(8,128)S(1)}, f32[480,128]{1,0:T(8,128)S(1)}, u32[]{:S(2)}, u32[]{:S(2)}) collective-permute-start(f32[480,128]{1,0:T(8,128)S(1)} %get-tuple-element.68), channel_id=1, source_target_pairs={{0,28},{4,0},{8,4},{12,8},{16,12},{20,16},{24,20},{28,24},{1,29},{... | collective-permute-start | bytes 737288 | tf_op jit(solution)/shard_map/ppermute | solution.py:702
  32.5 4.9 %collective-permute-done.10.refs_11_ = f32[24,128]{1,0:T(8,128)S(1)} collective-permute-done((f32[24,128]{1,0:T(8,128)S(1)}, f32[24,128]{1,0:T(8,128)S(1)}, u32[]{:S(2)}, u32[]{:S(2)}) %collective-permute-start.10) | collective-permute-done | bytes 12320 | tf_op jit(solution)/shard_map/ppermute | solution.py:702
  37.4 4.0 %shard_map.80 = (f32[512,256]{1,0:T(8,128)S(1)}, f32[512,256]{1,0:T(8,128)S(1)}, f32[512,256]{1,0:T(8,128)S(1)}, f32[256,256]{1,0:T(8,128)S(1)}, f32[256,256]{1,...) custom-call(s32[5]{0:T(128)S(1)} %pad_add_fusion.1.refs_0_, ...), custom_call_target="tpu_custom_call" | custom-call | tf_op jit(solution)/shard_map/pallas_call | solution.py:123
  41.4 2.6 %collective-permute-start.13 = (f32[256,128]{1,0:T(8,128)S(1)}, f32[256,128]{1,0:T(8,128)S(1)}, u32[]{:S(2)}, u32[]{:S(2)}) collective-permute-start(f32[256,128]{1,0:T(8,128)S(1)} %get-tuple-element.74), channel_id=1, source_target_pairs={{0,28},{4,0},{8,4},{12,8},{16,12},{20,16},{24,20},{28,24},{1,29},{... | collective-permute-start | bytes 393224 | tf_op jit(solution)/shard_map/ppermute | solution.py:702
  44.1 2.9 %collective-permute-start.15 = (f32[8,128]{1,0:T(8,128)S(1)}, f32[8,128]{1,0:T(8,128)S(1)}, u32[]{:S(2)}, u32[]{:S(2)}) collective-permute-start(f32[8,128]{1,0:T(8,128)S(1)} %get-tuple-element.76), channel_id=1, source_target_pairs={{0,24},{4,28},{8,0},{12,4},{16,8},{20,12},{24,16},{28,20},{1,25},{... | collective-permute-start | bytes 12296 | tf_op jit(solution)/shard_map/ppermute | solution.py:702
  47.0 1.6 %collective-permute-done.14.refs_8_ = f32[8,128]{1,0:T(8,128)S(1)} collective-permute-done((f32[8,128]{1,0:T(8,128)S(1)}, f32[8,128]{1,0:T(8,128)S(1)}, u32[]{:S(2)}, u32[]{:S(2)}) %collective-permute-start.14) | collective-permute-done | bytes 4128 | tf_op jit(solution)/shard_map/ppermute | solution.py:702
  48.7 3.6 %shard_map.81 = (f32[288,256]{1,0:T(8,128)S(1)}, f32[256,256]{1,0:T(8,128)S(1)}, f32[64,128]{1,0:T(8,128)S(1)}, f32[16,128]{1,0:T(8,128)S(1)}, f32[256,128]{1,0:...) custom-call(s32[5]{0:T(128)S(1)} %pad_add_fusion.1.refs_0_, ...), custom_call_target="tpu_custom_call" | custom-call | tf_op jit(solution)/shard_map/pallas_call | solution.py:123
  52.4 2.6 %collective-permute-start.17 = (f32[256,128]{1,0:T(8,128)S(1)}, f32[256,128]{1,0:T(8,128)S(1)}, u32[]{:S(2)}, u32[]{:S(2)}) collective-permute-start(f32[256,128]{1,0:T(8,128)S(1)} %get-tuple-element.95), channel_id=1, source_target_pairs={{0,28},{4,0},{8,4},{12,8},{16,12},{20,16},{24,20},{28,24},{1,29},{... | collective-permute-start | bytes 393224 | tf_op jit(solution)/shard_map/ppermute | solution.py:702
  55.0 2.0 %collective-permute-start.18 = (f32[8,128]{1,0:T(8,128)S(1)}, f32[8,128]{1,0:T(8,128)S(1)}, u32[]{:S(2)}, u32[]{:S(2)}) collective-permute-start(f32[8,128]{1,0:T(8,128)S(1)} %get-tuple-element.96), channel_id=1, source_target_pairs={{0,8},{4,12},{8,16},{12,20},{16,24},{20,28},{24,0},{28,4},{1,9},{5... | collective-permute-start | bytes 12296 | tf_op jit(solution)/shard_map/ppermute | solution.py:702
  57.9 2.1 %collective-permute-done.18.refs_8_ = f32[8,128]{1,0:T(8,128)S(1)} collective-permute-done((f32[8,128]{1,0:T(8,128)S(1)}, f32[8,128]{1,0:T(8,128)S(1)}, u32[]{:S(2)}, u32[]{:S(2)}) %collective-permute-start.18) | collective-permute-done | bytes 4128 | tf_op jit(solution)/shard_map/ppermute | solution.py:702
  60.6 3.6 %shard_map.82 = (f32[128,128]{1,0:T(8,128)S(1)}, f32[128,128]{1,0:T(8,128)S(1)}, f32[128,128]{1,0:T(8,128)S(1)}, f32[128,128]{1,0:T(8,128)S(1)}) custom-call(s32[5]{0:T(128)S(1)} %pad_add_fusion.1.refs_0_, f32[3,12]{1,0:T(4,128)S(1)} %stack.71.refs_1_, f32[256,256]{1,0:T(8,128)S(1)} %get-tuple-element.90.refs_2_, f32[64,128]{1,0:T(8,128)S(1)} %get-tuple-element.91.refs_3_, ...), custom_call_target="tpu_custom_call" | custom-call | tf_op jit(solution)/shard_map/pallas_call | solution.py:123
  65.2 1.7 %collective-permute-start.21 = (f32[128,128]{1,0:T(8,128)S(1)}, f32[128,128]{1,0:T(8,128)S(1)}, u32[]{:S(2)}, u32[]{:S(2)}) collective-permute-start(f32[128,128]{1,0:T(8,128)S(1)} %get-tuple-element.100), channel_id=1, source_target_pairs={{0,2},{1,3},{2,0},{3,1},{4,6},{5,7},{6,4},{7,5},{8,10},{9,11},{10,... | collective-permute-start | bytes 196616 | tf_op jit(solution)/shard_map/ppermute | solution.py:702
  66.9 1.9 %collective-permute-start.22 = (f32[128,128]{1,0:T(8,128)S(1)}, f32[128,128]{1,0:T(8,128)S(1)}, u32[]{:S(2)}, u32[]{:S(2)}) collective-permute-start(f32[128,128]{1,0:T(8,128)S(1)} %get-tuple-element.101), channel_id=1, source_target_pairs={{0,1},{1,2},{2,3},{3,0},{4,5},{5,6},{6,7},{7,4},{8,9},{9,10},{10,1... | collective-permute-start | bytes 196616 | tf_op jit(solution)/shard_map/ppermute | solution.py:702
  69.0 2.1 %collective-permute-done.21.refs_3_ = f32[128,128]{1,0:T(8,128)S(1)} collective-permute-done((f32[128,128]{1,0:T(8,128)S(1)}, f32[128,128]{1,0:T(8,128)S(1)}, u32[]{:S(2)}, u32[]{:S(2)}) %collective-permute-start.21) | collective-permute-done | bytes 65568 | tf_op jit(solution)/shard_map/ppermute | solution.py:702
  71.1 1.9 %collective-permute-done.22.refs_4_ = f32[128,128]{1,0:T(8,128)S(1)} collective-permute-done((f32[128,128]{1,0:T(8,128)S(1)}, f32[128,128]{1,0:T(8,128)S(1)}, u32[]{:S(2)}, u32[]{:S(2)}) %collective-permute-start.22) | collective-permute-done | bytes 65568 | tf_op jit(solution)/shard_map/ppermute | solution.py:702
  73.0 1.3 %shard_map.83 = (f32[4,16,512]{2,1,0:T(8,128)}, f32[4,16,512]{2,1,0:T(8,128)}) custom-call(s32[2]{0:T(128)S(1)} %pad_add_fusion.refs_0_, f32[128,128]{1,0:T(8,128)S(1)} %get-tuple-element.98.refs_1_, f32[128,128]{1,0:T(8,128)S(1)} %collective-permute-done.20.refs_2_, f32[128,128]{1,0:T(8,128)S(1)} %collective-permute-done.21.refs_3_, ...), custom_call_target="tpu_custom_call" | custom-call | tf_op jit(solution)/shard_map/pallas_call | solution.py:123
  (55 shorter events, 9.5 us)
Async XLA Ops:
  3.0 10.7 %collective-permute-start = (f32[80,256]{1,0:T(8,128)S(1)}, f32[80,256]{1,0:T(8,128)S(1)}, u32[]{:S(2)}, u32[]{:S(2)}) collective-permute-start(f32[80,256]{1,0:T(8,128)S(1)} %get-tuple-element.53), channel_id=1, source_target_pairs={{0,3},{1,0},{2,1},{3,2},{4,7},{5,4},{6,5},{7,6},{8,11},{9,8},{10,9... | collective-permute-start | bytes 245768 | tf_op jit(solution)/shard_map/ppermute | solution.py:702
  8.1 7.9 %collective-permute-start.1 = (f32[80,256]{1,0:T(8,128)S(1)}, f32[80,256]{1,0:T(8,128)S(1)}, u32[]{:S(2)}, u32[]{:S(2)}) collective-permute-start(f32[80,256]{1,0:T(8,128)S(1)} %get-tuple-element.54), channel_id=1, source_target_pairs={{0,2},{1,3},{2,0},{3,1},{4,6},{5,7},{6,4},{7,5},{8,10},{9,11},{10,... | collective-permute-start | bytes 245768 | tf_op jit(solution)/shard_map/ppermute | solution.py:702
  8.1 7.9 %collective-permute-start.2 = (f32[80,256]{1,0:T(8,128)S(1)}, f32[80,256]{1,0:T(8,128)S(1)}, u32[]{:S(2)}, u32[]{:S(2)}) collective-permute-start(f32[80,256]{1,0:T(8,128)S(1)} %get-tuple-element.55), channel_id=1, source_target_pairs={{0,1},{1,2},{2,3},{3,0},{4,5},{5,6},{6,7},{7,4},{8,9},{9,10},{10,1... | collective-permute-start | bytes 245768 | tf_op jit(solution)/shard_map/ppermute | solution.py:702
  9.1 3.9 %copy-start.2 = (f32[3]{0:T(128)S(1)}, f32[3]{0:T(128)}, u32[]{:S(2)}) copy-start(f32[3]{0:T(128)} %param.10) | copy-start | bytes 40
  9.1 10.2 %collective-permute-start.3 = (f32[128,256]{1,0:T(8,128)S(1)}, f32[128,256]{1,0:T(8,128)S(1)}, u32[]{:S(2)}, u32[]{:S(2)}) collective-permute-start(f32[128,256]{1,0:T(8,128)S(1)} %get-tuple-element.60), channel_id=1, source_target_pairs={{0,3},{1,0},{2,1},{3,2},{4,7},{5,4},{6,5},{7,6},{8,11},{9,8},{10,9... | collective-permute-start | bytes 393224 | tf_op jit(solution)/shard_map/ppermute | solution.py:702
  11.9 15.0 %collective-permute-start.4 = (f32[128,256]{1,0:T(8,128)S(1)}, f32[128,256]{1,0:T(8,128)S(1)}, u32[]{:S(2)}, u32[]{:S(2)}) collective-permute-start(f32[128,256]{1,0:T(8,128)S(1)} %get-tuple-element.61), channel_id=1, source_target_pairs={{0,2},{1,3},{2,0},{3,1},{4,6},{5,7},{6,4},{7,5},{8,10},{9,11},{10,... | collective-permute-start | bytes 393224 | tf_op jit(solution)/shard_map/ppermute | solution.py:702
  13.8 13.1 %collective-permute-start.5 = (f32[128,256]{1,0:T(8,128)S(1)}, f32[128,256]{1,0:T(8,128)S(1)}, u32[]{:S(2)}, u32[]{:S(2)}) collective-permute-start(f32[128,256]{1,0:T(8,128)S(1)} %get-tuple-element.62), channel_id=1, source_target_pairs={{0,1},{1,2},{2,3},{3,0},{4,5},{5,6},{6,7},{7,4},{8,9},{9,10},{10,1... | collective-permute-start | bytes 393224 | tf_op jit(solution)/shard_map/ppermute | solution.py:702
  16.9 13.8 %collective-permute-start.11 = (f32[24,128]{1,0:T(8,128)S(1)}, f32[24,128]{1,0:T(8,128)S(1)}, u32[]{:S(2)}, u32[]{:S(2)}) collective-permute-start(f32[24,128]{1,0:T(8,128)S(1)} %get-tuple-element.111), channel_id=1, source_target_pairs={{0,24},{4,28},{8,0},{12,4},{16,8},{20,12},{24,16},{28,20},{1,25},{... | collective-permute-start | bytes 36872 | tf_op jit(solution)/shard_map/ppermute | solution.py:702
  19.4 18.0 %collective-permute-start.6 = (f32[288,128]{1,0:T(8,128)S(1)}, f32[288,128]{1,0:T(8,128)S(1)}, u32[]{:S(2)}, u32[]{:S(2)}) collective-permute-start(f32[288,128]{1,0:T(8,128)S(1)} %get-tuple-element.65), channel_id=1, source_target_pairs={{0,4},{4,8},{8,12},{12,16},{16,20},{20,24},{24,28},{28,0},{1,5},{5... | collective-permute-start | bytes 442376 | tf_op jit(solution)/shard_map/ppermute | solution.py:702
  19.4 18.0 %collective-permute-start.7 = (f32[288,128]{1,0:T(8,128)S(1)}, f32[288,128]{1,0:T(8,128)S(1)}, u32[]{:S(2)}, u32[]{:S(2)}) collective-permute-start(f32[288,128]{1,0:T(8,128)S(1)} %get-tuple-element.66), channel_id=1, source_target_pairs={{0,28},{4,0},{8,4},{12,8},{16,12},{20,16},{24,20},{28,24},{1,29},{... | collective-permute-start | bytes 442376 | tf_op jit(solution)/shard_map/ppermute | solution.py:702
  27.9 9.5 %collective-permute-start.8 = (f32[480,128]{1,0:T(8,128)S(1)}, f32[480,128]{1,0:T(8,128)S(1)}, u32[]{:S(2)}, u32[]{:S(2)}) collective-permute-start(f32[480,128]{1,0:T(8,128)S(1)} %get-tuple-element.67), channel_id=1, source_target_pairs={{0,4},{4,8},{8,12},{12,16},{16,20},{20,24},{24,28},{28,0},{1,5},{5... | collective-permute-start | bytes 737288 | tf_op jit(solution)/shard_map/ppermute | solution.py:702
  28.0 9.4 %collective-permute-start.9 = (f32[480,128]{1,0:T(8,128)S(1)}, f32[480,128]{1,0:T(8,128)S(1)}, u32[]{:S(2)}, u32[]{:S(2)}) collective-permute-start(f32[480,128]{1,0:T(8,128)S(1)} %get-tuple-element.68), channel_id=1, source_target_pairs={{0,28},{4,0},{8,4},{12,8},{16,12},{20,16},{24,20},{28,24},{1,29},{... | collective-permute-start | bytes 737288 | tf_op jit(solution)/shard_map/ppermute | solution.py:702
  30.6 6.7 %collective-permute-start.10 = (f32[24,128]{1,0:T(8,128)S(1)}, f32[24,128]{1,0:T(8,128)S(1)}, u32[]{:S(2)}, u32[]{:S(2)}) collective-permute-start(f32[24,128]{1,0:T(8,128)S(1)} %get-tuple-element.112), channel_id=1, source_target_pairs={{0,8},{4,12},{8,16},{12,20},{16,24},{20,28},{24,0},{28,4},{1,9},{5... | collective-permute-start | bytes 36872 | tf_op jit(solution)/shard_map/ppermute | solution.py:702
  41.4 7.3 %collective-permute-start.12 = (f32[256,128]{1,0:T(8,128)S(1)}, f32[256,128]{1,0:T(8,128)S(1)}, u32[]{:S(2)}, u32[]{:S(2)}) collective-permute-start(f32[256,128]{1,0:T(8,128)S(1)} %get-tuple-element.73), channel_id=1, source_target_pairs={{0,4},{4,8},{8,12},{12,16},{16,20},{20,24},{24,28},{28,0},{1,5},{5... | collective-permute-start | bytes 393224 | tf_op jit(solution)/shard_map/ppermute | solution.py:702
  41.4 7.2 %collective-permute-start.13 = (f32[256,128]{1,0:T(8,128)S(1)}, f32[256,128]{1,0:T(8,128)S(1)}, u32[]{:S(2)}, u32[]{:S(2)}) collective-permute-start(f32[256,128]{1,0:T(8,128)S(1)} %get-tuple-element.74), channel_id=1, source_target_pairs={{0,28},{4,0},{8,4},{12,8},{16,12},{20,16},{24,20},{28,24},{1,29},{... | collective-permute-start | bytes 393224 | tf_op jit(solution)/shard_map/ppermute | solution.py:702
  44.1 4.5 %collective-permute-start.14 = (f32[8,128]{1,0:T(8,128)S(1)}, f32[8,128]{1,0:T(8,128)S(1)}, u32[]{:S(2)}, u32[]{:S(2)}) collective-permute-start(f32[8,128]{1,0:T(8,128)S(1)} %get-tuple-element.75), channel_id=1, source_target_pairs={{0,8},{4,12},{8,16},{12,20},{16,24},{20,28},{24,0},{28,4},{1,9},{5... | collective-permute-start | bytes 12296 | tf_op jit(solution)/shard_map/ppermute | solution.py:702
  44.1 4.6 %collective-permute-start.15 = (f32[8,128]{1,0:T(8,128)S(1)}, f32[8,128]{1,0:T(8,128)S(1)}, u32[]{:S(2)}, u32[]{:S(2)}) collective-permute-start(f32[8,128]{1,0:T(8,128)S(1)} %get-tuple-element.76), channel_id=1, source_target_pairs={{0,24},{4,28},{8,0},{12,4},{16,8},{20,12},{24,16},{28,20},{1,25},{... | collective-permute-start | bytes 12296 | tf_op jit(solution)/shard_map/ppermute | solution.py:702
  52.3 8.3 %collective-permute-start.16 = (f32[256,128]{1,0:T(8,128)S(1)}, f32[256,128]{1,0:T(8,128)S(1)}, u32[]{:S(2)}, u32[]{:S(2)}) collective-permute-start(f32[256,128]{1,0:T(8,128)S(1)} %get-tuple-element.94), channel_id=1, source_target_pairs={{0,4},{4,8},{8,12},{12,16},{16,20},{20,24},{24,28},{28,0},{1,5},{5... | collective-permute-start | bytes 393224 | tf_op jit(solution)/shard_map/ppermute | solution.py:702
  52.4 8.2 %collective-permute-start.17 = (f32[256,128]{1,0:T(8,128)S(1)}, f32[256,128]{1,0:T(8,128)S(1)}, u32[]{:S(2)}, u32[]{:S(2)}) collective-permute-start(f32[256,128]{1,0:T(8,128)S(1)} %get-tuple-element.95), channel_id=1, source_target_pairs={{0,28},{4,0},{8,4},{12,8},{16,12},{20,16},{24,20},{28,24},{1,29},{... | collective-permute-start | bytes 393224 | tf_op jit(solution)/shard_map/ppermute | solution.py:702
  55.0 5.0 %collective-permute-start.18 = (f32[8,128]{1,0:T(8,128)S(1)}, f32[8,128]{1,0:T(8,128)S(1)}, u32[]{:S(2)}, u32[]{:S(2)}) collective-permute-start(f32[8,128]{1,0:T(8,128)S(1)} %get-tuple-element.96), channel_id=1, source_target_pairs={{0,8},{4,12},{8,16},{12,20},{16,24},{20,28},{24,0},{28,4},{1,9},{5... | collective-permute-start | bytes 12296 | tf_op jit(solution)/shard_map/ppermute | solution.py:702
  57.0 3.6 %collective-permute-start.19 = (f32[8,128]{1,0:T(8,128)S(1)}, f32[8,128]{1,0:T(8,128)S(1)}, u32[]{:S(2)}, u32[]{:S(2)}) collective-permute-start(f32[8,128]{1,0:T(8,128)S(1)} %get-tuple-element.97), channel_id=1, source_target_pairs={{0,24},{4,28},{8,0},{12,4},{16,8},{20,12},{24,16},{28,20},{1,25},{... | collective-permute-start | bytes 12296 | tf_op jit(solution)/shard_map/ppermute | solution.py:702
  64.2 4.8 %collective-permute-start.20 = (f32[128,128]{1,0:T(8,128)S(1)}, f32[128,128]{1,0:T(8,128)S(1)}, u32[]{:S(2)}, u32[]{:S(2)}) collective-permute-start(f32[128,128]{1,0:T(8,128)S(1)} %get-tuple-element.99), channel_id=1, source_target_pairs={{0,3},{1,0},{2,1},{3,2},{4,7},{5,4},{6,5},{7,6},{8,11},{9,8},{10,9... | collective-permute-start | bytes 196616 | tf_op jit(solution)/shard_map/ppermute | solution.py:702
  65.2 5.9 %collective-permute-start.21 = (f32[128,128]{1,0:T(8,128)S(1)}, f32[128,128]{1,0:T(8,128)S(1)}, u32[]{:S(2)}, u32[]{:S(2)}) collective-permute-start(f32[128,128]{1,0:T(8,128)S(1)} %get-tuple-element.100), channel_id=1, source_target_pairs={{0,2},{1,3},{2,0},{3,1},{4,6},{5,7},{6,4},{7,5},{8,10},{9,11},{10,... | collective-permute-start | bytes 196616 | tf_op jit(solution)/shard_map/ppermute | solution.py:702
  66.9 6.1 %collective-permute-start.22 = (f32[128,128]{1,0:T(8,128)S(1)}, f32[128,128]{1,0:T(8,128)S(1)}, u32[]{:S(2)}, u32[]{:S(2)}) collective-permute-start(f32[128,128]{1,0:T(8,128)S(1)} %get-tuple-element.101), channel_id=1, source_target_pairs={{0,1},{1,2},{2,3},{3,0},{4,5},{5,6},{6,7},{7,4},{8,9},{9,10},{10,1... | collective-permute-start | bytes 196616 | tf_op jit(solution)/shard_map/ppermute | solution.py:702
  (2 other events, 4.6 us)

commit v3 on v2

--- a/solution.py
+++ b/solution.py
@@ -308,12 +308,12 @@
             y[r, :] = held[q] + nd
 
     ahead = {j: () for j in range(1, MAXDEG)}
-    ahead[1], ahead[2], ahead[3] = (1, 2), (3, 4), (5,)
+    ahead[1], ahead[2] = (1, 2), (3, 4, 5)
 
     def beside(j):
         for k in ahead[j]:
             small_sweep(tab, k, grids)
-        if j == 4:
+        if j == 3:
             coarse_correction(g, idx[0], mid[4], low[4], zd)
 
     fine_sweep(1)
@@ -325,7 +325,7 @@
             fine_sweep(j)
             beside(j)
 
-        if j < 5:
+        if j < 4:
 
             @pl.when(j >= idx[2])
             def _(j=j):

time: 74.5 us -> 74.9 us (level)
  no operation moved by 1% of the time
where the time goes in v3:
time: 74.9 us; the launch traced here: 74.7 us
  starting transfers between devices  34.5 us (46%)
  waiting for transfers between devices  20.5 us (27%)
  Pallas kernels  16 us (21%)
  local copies, waits for them, and re-layouts  1.78 us (2%)
  other arithmetic  1.24 us (2%)
  between operations  0.77 us (1%)
    ppermute x23, starting transfers between devices, ring(): lax.ppermute(value, axis, [(i, (i - by) % peers) for i in range(peers)])  34.5 us
    ppermute x23, waiting for transfers between devices, ring(): lax.ppermute(value, axis, [(i, (i - by) % peers) for i in range(peers)])  20.5 us
    pallas_call x7, Pallas kernels, vmem_call(): pl.pallas_call(kernel, out_shape=[jax.ShapeDtypeStruct(o, F32) for o in o...  16 us
  transfers between devices with their start and end apart: 23, of which 10 were waited for; matrix products, arithmetic and copies ran while one was open for 2% of the time, Pallas kernels for 2%

profile of v3, /device:TPU:0, one launch (start us, length us, event | category | flops | bytes accessed | tf_op | source)
XLA Modules:
  0.0 74.7 jit_solution(1146828226867690091)
XLA Ops:
  1.8 1.2 %shard_map.77 = (f32[80,256]{1,0:T(8,128)S(1)}, f32[80,256]{1,0:T(8,128)S(1)}, f32[80,256]{1,0:T(8,128)S(1)}, f32[80,256]{1,0:T(8,128)S(1)}, f32[128,256]{1,0:T(...) custom-call(s32[2]{0:T(128)S(1)} %pad_add_fusion.refs_0_, ...), custom_call_target="tpu_custom_call" | custom-call | tf_op jit(solution)/shard_map/pallas_call | solution.py:123
  3.0 5.1 %collective-permute-start = (f32[80,256]{1,0:T(8,128)S(1)}, f32[80,256]{1,0:T(8,128)S(1)}, u32[]{:S(2)}, u32[]{:S(2)}) collective-permute-start(f32[80,256]{1,0:T(8,128)S(1)} %get-tuple-element.53), channel_id=1, source_target_pairs={{0,3},{1,0},{2,1},{3,2},{4,7},{5,4},{6,5},{7,6},{8,11},{9,8},{10,9... | collective-permute-start | bytes 245768 | tf_op jit(solution)/shard_map/ppermute | solution.py:702
  9.1 2.8 %collective-permute-start.3 = (f32[128,256]{1,0:T(8,128)S(1)}, f32[128,256]{1,0:T(8,128)S(1)}, u32[]{:S(2)}, u32[]{:S(2)}) collective-permute-start(f32[128,256]{1,0:T(8,128)S(1)} %get-tuple-element.60), channel_id=1, source_target_pairs={{0,3},{1,0},{2,1},{3,2},{4,7},{5,4},{6,5},{7,6},{8,11},{9,8},{10,9... | collective-permute-start | bytes 393224 | tf_op jit(solution)/shard_map/ppermute | solution.py:702
  11.9 1.1 %collective-permute-start.4 = (f32[128,256]{1,0:T(8,128)S(1)}, f32[128,256]{1,0:T(8,128)S(1)}, u32[]{:S(2)}, u32[]{:S(2)}) collective-permute-start(f32[128,256]{1,0:T(8,128)S(1)} %get-tuple-element.61), channel_id=1, source_target_pairs={{0,2},{1,3},{2,0},{3,1},{4,6},{5,7},{6,4},{7,5},{8,10},{9,11},{10,... | collective-permute-start | bytes 393224 | tf_op jit(solution)/shard_map/ppermute | solution.py:702
  13.8 2.2 %collective-permute-done.1.refs_3_ = f32[80,256]{1,0:T(8,128)S(1)} collective-permute-done((f32[80,256]{1,0:T(8,128)S(1)}, f32[80,256]{1,0:T(8,128)S(1)}, u32[]{:S(2)}, u32[]{:S(2)}) %collective-permute-start.1) | collective-permute-done | bytes 81952 | tf_op jit(solution)/shard_map/ppermute | solution.py:702
  16.9 2.5 %collective-permute-start.11 = (f32[24,128]{1,0:T(8,128)S(1)}, f32[24,128]{1,0:T(8,128)S(1)}, u32[]{:S(2)}, u32[]{:S(2)}) collective-permute-start(f32[24,128]{1,0:T(8,128)S(1)} %get-tuple-element.111), channel_id=1, source_target_pairs={{0,24},{4,28},{8,0},{12,4},{16,8},{20,12},{24,16},{28,20},{1,25},{... | collective-permute-start | bytes 36872 | tf_op jit(solution)/shard_map/ppermute | solution.py:702
  19.4 2.6 %collective-permute-start.7 = (f32[288,128]{1,0:T(8,128)S(1)}, f32[288,128]{1,0:T(8,128)S(1)}, u32[]{:S(2)}, u32[]{:S(2)}) collective-permute-start(f32[288,128]{1,0:T(8,128)S(1)} %get-tuple-element.66), channel_id=1, source_target_pairs={{0,28},{4,0},{8,4},{12,8},{16,12},{20,16},{24,20},{28,24},{1,29},{... | collective-permute-start | bytes 442376 | tf_op jit(solution)/shard_map/ppermute | solution.py:702
  22.0 4.9 %collective-permute-done.4.refs_3_ = f32[128,256]{1,0:T(8,128)S(1)} collective-permute-done((f32[128,256]{1,0:T(8,128)S(1)}, f32[128,256]{1,0:T(8,128)S(1)}, u32[]{:S(2)}, u32[]{:S(2)}) %collective-permute-start.4) | collective-permute-done | bytes 131104 | tf_op jit(solution)/shard_map/ppermute | solution.py:702
  28.0 2.6 %collective-permute-start.9 = (f32[480,128]{1,0:T(8,128)S(1)}, f32[480,128]{1,0:T(8,128)S(1)}, u32[]{:S(2)}, u32[]{:S(2)}) collective-permute-start(f32[480,128]{1,0:T(8,128)S(1)} %get-tuple-element.68), channel_id=1, source_target_pairs={{0,28},{4,0},{8,4},{12,8},{16,12},{20,16},{24,20},{28,24},{1,29},{... | collective-permute-start | bytes 737288 | tf_op jit(solution)/shard_map/ppermute | solution.py:702
  32.5 4.9 %collective-permute-done.10.refs_11_ = f32[24,128]{1,0:T(8,128)S(1)} collective-permute-done((f32[24,128]{1,0:T(8,128)S(1)}, f32[24,128]{1,0:T(8,128)S(1)}, u32[]{:S(2)}, u32[]{:S(2)}) %collective-permute-start.10) | collective-permute-done | bytes 12320 | tf_op jit(solution)/shard_map/ppermute | solution.py:702
  37.4 4.0 %shard_map.80 = (f32[512,256]{1,0:T(8,128)S(1)}, f32[512,256]{1,0:T(8,128)S(1)}, f32[512,256]{1,0:T(8,128)S(1)}, f32[256,256]{1,0:T(8,128)S(1)}, f32[256,256]{1,...) custom-call(s32[5]{0:T(128)S(1)} %pad_add_fusion.1.refs_0_, ...), custom_call_target="tpu_custom_call" | custom-call | tf_op jit(solution)/shard_map/pallas_call | solution.py:123
  41.5 2.6 %collective-permute-start.13 = (f32[256,128]{1,0:T(8,128)S(1)}, f32[256,128]{1,0:T(8,128)S(1)}, u32[]{:S(2)}, u32[]{:S(2)}) collective-permute-start(f32[256,128]{1,0:T(8,128)S(1)} %get-tuple-element.74), channel_id=1, source_target_pairs={{0,28},{4,0},{8,4},{12,8},{16,12},{20,16},{24,20},{28,24},{1,29},{... | collective-permute-start | bytes 393224 | tf_op jit(solution)/shard_map/ppermute | solution.py:702
  44.1 2.9 %collective-permute-start.15 = (f32[8,128]{1,0:T(8,128)S(1)}, f32[8,128]{1,0:T(8,128)S(1)}, u32[]{:S(2)}, u32[]{:S(2)}) collective-permute-start(f32[8,128]{1,0:T(8,128)S(1)} %get-tuple-element.76), channel_id=1, source_target_pairs={{0,24},{4,28},{8,0},{12,4},{16,8},{20,12},{24,16},{28,20},{1,25},{... | collective-permute-start | bytes 12296 | tf_op jit(solution)/shard_map/ppermute | solution.py:702
  47.0 1.6 %collective-permute-done.14.refs_8_ = f32[8,128]{1,0:T(8,128)S(1)} collective-permute-done((f32[8,128]{1,0:T(8,128)S(1)}, f32[8,128]{1,0:T(8,128)S(1)}, u32[]{:S(2)}, u32[]{:S(2)}) %collective-permute-start.14) | collective-permute-done | bytes 4128 | tf_op jit(solution)/shard_map/ppermute | solution.py:702
  48.7 3.7 %shard_map.81 = (f32[288,256]{1,0:T(8,128)S(1)}, f32[256,256]{1,0:T(8,128)S(1)}, f32[64,128]{1,0:T(8,128)S(1)}, f32[16,128]{1,0:T(8,128)S(1)}, f32[256,128]{1,0:...) custom-call(s32[5]{0:T(128)S(1)} %pad_add_fusion.1.refs_0_, ...), custom_call_target="tpu_custom_call" | custom-call | tf_op jit(solution)/shard_map/pallas_call | solution.py:123
  52.5 2.6 %collective-permute-start.17 = (f32[256,128]{1,0:T(8,128)S(1)}, f32[256,128]{1,0:T(8,128)S(1)}, u32[]{:S(2)}, u32[]{:S(2)}) collective-permute-start(f32[256,128]{1,0:T(8,128)S(1)} %get-tuple-element.95), channel_id=1, source_target_pairs={{0,28},{4,0},{8,4},{12,8},{16,12},{20,16},{24,20},{28,24},{1,29},{... | collective-permute-start | bytes 393224 | tf_op jit(solution)/shard_map/ppermute | solution.py:702
  55.1 2.0 %collective-permute-start.18 = (f32[8,128]{1,0:T(8,128)S(1)}, f32[8,128]{1,0:T(8,128)S(1)}, u32[]{:S(2)}, u32[]{:S(2)}) collective-permute-start(f32[8,128]{1,0:T(8,128)S(1)} %get-tuple-element.96), channel_id=1, source_target_pairs={{0,8},{4,12},{8,16},{12,20},{16,24},{20,28},{24,0},{28,4},{1,9},{5... | collective-permute-start | bytes 12296 | tf_op jit(solution)/shard_map/ppermute | solution.py:702
  58.1 2.1 %collective-permute-done.18.refs_8_ = f32[8,128]{1,0:T(8,128)S(1)} collective-permute-done((f32[8,128]{1,0:T(8,128)S(1)}, f32[8,128]{1,0:T(8,128)S(1)}, u32[]{:S(2)}, u32[]{:S(2)}) %collective-permute-start.18) | collective-permute-done | bytes 4128 | tf_op jit(solution)/shard_map/ppermute | solution.py:702
  60.7 3.8 %shard_map.82 = (f32[128,128]{1,0:T(8,128)S(1)}, f32[128,128]{1,0:T(8,128)S(1)}, f32[128,128]{1,0:T(8,128)S(1)}, f32[128,128]{1,0:T(8,128)S(1)}) custom-call(s32[5]{0:T(128)S(1)} %pad_add_fusion.1.refs_0_, f32[3,12]{1,0:T(4,128)S(1)} %stack.71.refs_1_, f32[256,256]{1,0:T(8,128)S(1)} %get-tuple-element.90.refs_2_, f32[64,128]{1,0:T(8,128)S(1)} %get-tuple-element.91.refs_3_, ...), custom_call_target="tpu_custom_call" | custom-call | tf_op jit(solution)/shard_map/pallas_call | solution.py:123
  65.6 1.7 %collective-permute-start.21 = (f32[128,128]{1,0:T(8,128)S(1)}, f32[128,128]{1,0:T(8,128)S(1)}, u32[]{:S(2)}, u32[]{:S(2)}) collective-permute-start(f32[128,128]{1,0:T(8,128)S(1)} %get-tuple-element.100), channel_id=1, source_target_pairs={{0,2},{1,3},{2,0},{3,1},{4,6},{5,7},{6,4},{7,5},{8,10},{9,11},{10,... | collective-permute-start | bytes 196616 | tf_op jit(solution)/shard_map/ppermute | solution.py:702
  67.3 1.9 %collective-permute-start.22 = (f32[128,128]{1,0:T(8,128)S(1)}, f32[128,128]{1,0:T(8,128)S(1)}, u32[]{:S(2)}, u32[]{:S(2)}) collective-permute-start(f32[128,128]{1,0:T(8,128)S(1)} %get-tuple-element.101), channel_id=1, source_target_pairs={{0,1},{1,2},{2,3},{3,0},{4,5},{5,6},{6,7},{7,4},{8,9},{9,10},{10,1... | collective-permute-start | bytes 196616 | tf_op jit(solution)/shard_map/ppermute | solution.py:702
  69.3 2.1 %collective-permute-done.21.refs_3_ = f32[128,128]{1,0:T(8,128)S(1)} collective-permute-done((f32[128,128]{1,0:T(8,128)S(1)}, f32[128,128]{1,0:T(8,128)S(1)}, u32[]{:S(2)}, u32[]{:S(2)}) %collective-permute-start.21) | collective-permute-done | bytes 65568 | tf_op jit(solution)/shard_map/ppermute | solution.py:702
  71.4 1.9 %collective-permute-done.22.refs_4_ = f32[128,128]{1,0:T(8,128)S(1)} collective-permute-done((f32[128,128]{1,0:T(8,128)S(1)}, f32[128,128]{1,0:T(8,128)S(1)}, u32[]{:S(2)}, u32[]{:S(2)}) %collective-permute-start.22) | collective-permute-done | bytes 65568 | tf_op jit(solution)/shard_map/ppermute | solution.py:702
  73.4 1.3 %shard_map.83 = (f32[4,16,512]{2,1,0:T(8,128)}, f32[4,16,512]{2,1,0:T(8,128)}) custom-call(s32[2]{0:T(128)S(1)} %pad_add_fusion.refs_0_, f32[128,128]{1,0:T(8,128)S(1)} %get-tuple-element.98.refs_1_, f32[128,128]{1,0:T(8,128)S(1)} %collective-permute-done.20.refs_2_, f32[128,128]{1,0:T(8,128)S(1)} %collective-permute-done.21.refs_3_, ...), custom_call_target="tpu_custom_call" | custom-call | tf_op jit(solution)/shard_map/pallas_call | solution.py:123
  (55 shorter events, 9.5 us)
Async XLA Ops:
  3.0 10.7 %collective-permute-start = (f32[80,256]{1,0:T(8,128)S(1)}, f32[80,256]{1,0:T(8,128)S(1)}, u32[]{:S(2)}, u32[]{:S(2)}) collective-permute-start(f32[80,256]{1,0:T(8,128)S(1)} %get-tuple-element.53), channel_id=1, source_target_pairs={{0,3},{1,0},{2,1},{3,2},{4,7},{5,4},{6,5},{7,6},{8,11},{9,8},{10,9... | collective-permute-start | bytes 245768 | tf_op jit(solution)/shard_map/ppermute | solution.py:702
  8.1 7.9 %collective-permute-start.1 = (f32[80,256]{1,0:T(8,128)S(1)}, f32[80,256]{1,0:T(8,128)S(1)}, u32[]{:S(2)}, u32[]{:S(2)}) collective-permute-start(f32[80,256]{1,0:T(8,128)S(1)} %get-tuple-element.54), channel_id=1, source_target_pairs={{0,2},{1,3},{2,0},{3,1},{4,6},{5,7},{6,4},{7,5},{8,10},{9,11},{10,... | collective-permute-start | bytes 245768 | tf_op jit(solution)/shard_map/ppermute | solution.py:702
  8.1 7.9 %collective-permute-start.2 = (f32[80,256]{1,0:T(8,128)S(1)}, f32[80,256]{1,0:T(8,128)S(1)}, u32[]{:S(2)}, u32[]{:S(2)}) collective-permute-start(f32[80,256]{1,0:T(8,128)S(1)} %get-tuple-element.55), channel_id=1, source_target_pairs={{0,1},{1,2},{2,3},{3,0},{4,5},{5,6},{6,7},{7,4},{8,9},{9,10},{10,1... | collective-permute-start | bytes 245768 | tf_op jit(solution)/shard_map/ppermute | solution.py:702
  9.1 3.9 %copy-start.2 = (f32[3]{0:T(128)S(1)}, f32[3]{0:T(128)}, u32[]{:S(2)}) copy-start(f32[3]{0:T(128)} %param.10) | copy-start | bytes 40
  9.1 10.2 %collective-permute-start.3 = (f32[128,256]{1,0:T(8,128)S(1)}, f32[128,256]{1,0:T(8,128)S(1)}, u32[]{:S(2)}, u32[]{:S(2)}) collective-permute-start(f32[128,256]{1,0:T(8,128)S(1)} %get-tuple-element.60), channel_id=1, source_target_pairs={{0,3},{1,0},{2,1},{3,2},{4,7},{5,4},{6,5},{7,6},{8,11},{9,8},{10,9... | collective-permute-start | bytes 393224 | tf_op jit(solution)/shard_map/ppermute | solution.py:702
  11.9 15.0 %collective-permute-start.4 = (f32[128,256]{1,0:T(8,128)S(1)}, f32[128,256]{1,0:T(8,128)S(1)}, u32[]{:S(2)}, u32[]{:S(2)}) collective-permute-start(f32[128,256]{1,0:T(8,128)S(1)} %get-tuple-element.61), channel_id=1, source_target_pairs={{0,2},{1,3},{2,0},{3,1},{4,6},{5,7},{6,4},{7,5},{8,10},{9,11},{10,... | collective-permute-start | bytes 393224 | tf_op jit(solution)/shard_map/ppermute | solution.py:702
  13.8 13.1 %collective-permute-start.5 = (f32[128,256]{1,0:T(8,128)S(1)}, f32[128,256]{1,0:T(8,128)S(1)}, u32[]{:S(2)}, u32[]{:S(2)}) collective-permute-start(f32[128,256]{1,0:T(8,128)S(1)} %get-tuple-element.62), channel_id=1, source_target_pairs={{0,1},{1,2},{2,3},{3,0},{4,5},{5,6},{6,7},{7,4},{8,9},{9,10},{10,1... | collective-permute-start | bytes 393224 | tf_op jit(solution)/shard_map/ppermute | solution.py:702
  16.9 13.8 %collective-permute-start.11 = (f32[24,128]{1,0:T(8,128)S(1)}, f32[24,128]{1,0:T(8,128)S(1)}, u32[]{:S(2)}, u32[]{:S(2)}) collective-permute-start(f32[24,128]{1,0:T(8,128)S(1)} %get-tuple-element.111), channel_id=1, source_target_pairs={{0,24},{4,28},{8,0},{12,4},{16,8},{20,12},{24,16},{28,20},{1,25},{... | collective-permute-start | bytes 36872 | tf_op jit(solution)/shard_map/ppermute | solution.py:702
  19.4 18.0 %collective-permute-start.6 = (f32[288,128]{1,0:T(8,128)S(1)}, f32[288,128]{1,0:T(8,128)S(1)}, u32[]{:S(2)}, u32[]{:S(2)}) collective-permute-start(f32[288,128]{1,0:T(8,128)S(1)} %get-tuple-element.65), channel_id=1, source_target_pairs={{0,4},{4,8},{8,12},{12,16},{16,20},{20,24},{24,28},{28,0},{1,5},{5... | collective-permute-start | bytes 442376 | tf_op jit(solution)/shard_map/ppermute | solution.py:702
  19.4 18.0 %collective-permute-start.7 = (f32[288,128]{1,0:T(8,128)S(1)}, f32[288,128]{1,0:T(8,128)S(1)}, u32[]{:S(2)}, u32[]{:S(2)}) collective-permute-start(f32[288,128]{1,0:T(8,128)S(1)} %get-tuple-element.66), channel_id=1, source_target_pairs={{0,28},{4,0},{8,4},{12,8},{16,12},{20,16},{24,20},{28,24},{1,29},{... | collective-permute-start | bytes 442376 | tf_op jit(solution)/shard_map/ppermute | solution.py:702
  27.9 9.5 %collective-permute-start.8 = (f32[480,128]{1,0:T(8,128)S(1)}, f32[480,128]{1,0:T(8,128)S(1)}, u32[]{:S(2)}, u32[]{:S(2)}) collective-permute-start(f32[480,128]{1,0:T(8,128)S(1)} %get-tuple-element.67), channel_id=1, source_target_pairs={{0,4},{4,8},{8,12},{12,16},{16,20},{20,24},{24,28},{28,0},{1,5},{5... | collective-permute-start | bytes 737288 | tf_op jit(solution)/shard_map/ppermute | solution.py:702
  28.0 9.4 %collective-permute-start.9 = (f32[480,128]{1,0:T(8,128)S(1)}, f32[480,128]{1,0:T(8,128)S(1)}, u32[]{:S(2)}, u32[]{:S(2)}) collective-permute-start(f32[480,128]{1,0:T(8,128)S(1)} %get-tuple-element.68), channel_id=1, source_target_pairs={{0,28},{4,0},{8,4},{12,8},{16,12},{20,16},{24,20},{28,24},{1,29},{... | collective-permute-start | bytes 737288 | tf_op jit(solution)/shard_map/ppermute | solution.py:702
  30.6 6.7 %collective-permute-start.10 = (f32[24,128]{1,0:T(8,128)S(1)}, f32[24,128]{1,0:T(8,128)S(1)}, u32[]{:S(2)}, u32[]{:S(2)}) collective-permute-start(f32[24,128]{1,0:T(8,128)S(1)} %get-tuple-element.112), channel_id=1, source_target_pairs={{0,8},{4,12},{8,16},{12,20},{16,24},{20,28},{24,0},{28,4},{1,9},{5... | collective-permute-start | bytes 36872 | tf_op jit(solution)/shard_map/ppermute | solution.py:702
  41.4 7.3 %collective-permute-start.12 = (f32[256,128]{1,0:T(8,128)S(1)}, f32[256,128]{1,0:T(8,128)S(1)}, u32[]{:S(2)}, u32[]{:S(2)}) collective-permute-start(f32[256,128]{1,0:T(8,128)S(1)} %get-tuple-element.73), channel_id=1, source_target_pairs={{0,4},{4,8},{8,12},{12,16},{16,20},{20,24},{24,28},{28,0},{1,5},{5... | collective-permute-start | bytes 393224 | tf_op jit(solution)/shard_map/ppermute | solution.py:702
  41.5 7.2 %collective-permute-start.13 = (f32[256,128]{1,0:T(8,128)S(1)}, f32[256,128]{1,0:T(8,128)S(1)}, u32[]{:S(2)}, u32[]{:S(2)}) collective-permute-start(f32[256,128]{1,0:T(8,128)S(1)} %get-tuple-element.74), channel_id=1, source_target_pairs={{0,28},{4,0},{8,4},{12,8},{16,12},{20,16},{24,20},{28,24},{1,29},{... | collective-permute-start | bytes 393224 | tf_op jit(solution)/shard_map/ppermute | solution.py:702
  44.1 4.5 %collective-permute-start.14 = (f32[8,128]{1,0:T(8,128)S(1)}, f32[8,128]{1,0:T(8,128)S(1)}, u32[]{:S(2)}, u32[]{:S(2)}) collective-permute-start(f32[8,128]{1,0:T(8,128)S(1)} %get-tuple-element.75), channel_id=1, source_target_pairs={{0,8},{4,12},{8,16},{12,20},{16,24},{20,28},{24,0},{28,4},{1,9},{5... | collective-permute-start | bytes 12296 | tf_op jit(solution)/shard_map/ppermute | solution.py:702
  44.1 4.6 %collective-permute-start.15 = (f32[8,128]{1,0:T(8,128)S(1)}, f32[8,128]{1,0:T(8,128)S(1)}, u32[]{:S(2)}, u32[]{:S(2)}) collective-permute-start(f32[8,128]{1,0:T(8,128)S(1)} %get-tuple-element.76), channel_id=1, source_target_pairs={{0,24},{4,28},{8,0},{12,4},{16,8},{20,12},{24,16},{28,20},{1,25},{... | collective-permute-start | bytes 12296 | tf_op jit(solution)/shard_map/ppermute | solution.py:702
  52.4 8.3 %collective-permute-start.16 = (f32[256,128]{1,0:T(8,128)S(1)}, f32[256,128]{1,0:T(8,128)S(1)}, u32[]{:S(2)}, u32[]{:S(2)}) collective-permute-start(f32[256,128]{1,0:T(8,128)S(1)} %get-tuple-element.94), channel_id=1, source_target_pairs={{0,4},{4,8},{8,12},{12,16},{16,20},{20,24},{24,28},{28,0},{1,5},{5... | collective-permute-start | bytes 393224 | tf_op jit(solution)/shard_map/ppermute | solution.py:702
  52.5 8.2 %collective-permute-start.17 = (f32[256,128]{1,0:T(8,128)S(1)}, f32[256,128]{1,0:T(8,128)S(1)}, u32[]{:S(2)}, u32[]{:S(2)}) collective-permute-start(f32[256,128]{1,0:T(8,128)S(1)} %get-tuple-element.95), channel_id=1, source_target_pairs={{0,28},{4,0},{8,4},{12,8},{16,12},{20,16},{24,20},{28,24},{1,29},{... | collective-permute-start | bytes 393224 | tf_op jit(solution)/shard_map/ppermute | solution.py:702
  55.1 5.0 %collective-permute-start.18 = (f32[8,128]{1,0:T(8,128)S(1)}, f32[8,128]{1,0:T(8,128)S(1)}, u32[]{:S(2)}, u32[]{:S(2)}) collective-permute-start(f32[8,128]{1,0:T(8,128)S(1)} %get-tuple-element.96), channel_id=1, source_target_pairs={{0,8},{4,12},{8,16},{12,20},{16,24},{20,28},{24,0},{28,4},{1,9},{5... | collective-permute-start | bytes 12296 | tf_op jit(solution)/shard_map/ppermute | solution.py:702
  57.1 3.6 %collective-permute-start.19 = (f32[8,128]{1,0:T(8,128)S(1)}, f32[8,128]{1,0:T(8,128)S(1)}, u32[]{:S(2)}, u32[]{:S(2)}) collective-permute-start(f32[8,128]{1,0:T(8,128)S(1)} %get-tuple-element.97), channel_id=1, source_target_pairs={{0,24},{4,28},{8,0},{12,4},{16,8},{20,12},{24,16},{28,20},{1,25},{... | collective-permute-start | bytes 12296 | tf_op jit(solution)/shard_map/ppermute | solution.py:702
  64.6 4.8 %collective-permute-start.20 = (f32[128,128]{1,0:T(8,128)S(1)}, f32[128,128]{1,0:T(8,128)S(1)}, u32[]{:S(2)}, u32[]{:S(2)}) collective-permute-start(f32[128,128]{1,0:T(8,128)S(1)} %get-tuple-element.99), channel_id=1, source_target_pairs={{0,3},{1,0},{2,1},{3,2},{4,7},{5,4},{6,5},{7,6},{8,11},{9,8},{10,9... | collective-permute-start | bytes 196616 | tf_op jit(solution)/shard_map/ppermute | solution.py:702
  65.6 5.9 %collective-permute-start.21 = (f32[128,128]{1,0:T(8,128)S(1)}, f32[128,128]{1,0:T(8,128)S(1)}, u32[]{:S(2)}, u32[]{:S(2)}) collective-permute-start(f32[128,128]{1,0:T(8,128)S(1)} %get-tuple-element.100), channel_id=1, source_target_pairs={{0,2},{1,3},{2,0},{3,1},{4,6},{5,7},{6,4},{7,5},{8,10},{9,11},{10,... | collective-permute-start | bytes 196616 | tf_op jit(solution)/shard_map/ppermute | solution.py:702
  67.3 6.1 %collective-permute-start.22 = (f32[128,128]{1,0:T(8,128)S(1)}, f32[128,128]{1,0:T(8,128)S(1)}, u32[]{:S(2)}, u32[]{:S(2)}) collective-permute-start(f32[128,128]{1,0:T(8,128)S(1)} %get-tuple-element.101), channel_id=1, source_target_pairs={{0,1},{1,2},{2,3},{3,0},{4,5},{5,6},{6,7},{7,4},{8,9},{9,10},{10,1... | collective-permute-start | bytes 196616 | tf_op jit(solution)/shard_map/ppermute | solution.py:702
  (2 other events, 4.6 us)
